TPU v7x, 512 devices: a whole 4x4x16 slice. The times are simulated.
512 devices in a mesh: dp: 2 (over x_lo), seq: 32 (over z, core), tensor: 8 (over y, x_hi).
Axes of the slice: x: 4 (x_hi: 2, x_lo: 2; x = x_hi * 2 + x_lo), y: 4, z: 16, core: 2. Of those that a mesh axis runs over, the one named last changes fastest.
Arguments:
- queries: bfloat16 [2, 4096, 3072], P('dp', 'seq', 'tensor'), may hold values from -24 to 24
- keys: bfloat16 [2, 8192, 3072], P('dp', 'seq', 'tensor'), may hold values from -8 to 8
- values: bfloat16 [2, 8192, 3072], P('dp', 'seq', 'tensor'), may hold values from -160 to 160
- grad_out: bfloat16 [2, 4096, 3072], P('dp', 'seq', 'tensor'), may hold values from -60 to 60
- gain: float32 [3072], P('tensor'), may hold values from 0.1 to 1.9
- band_start: int32 [2, 32], P('dp', 'seq'), may hold values from 0 to 62, as said below
- band_end: int32 [2, 32], P('dp', 'seq'), may hold values from 6 to 64
Outputs:
- attended: bfloat16 [2, 4096, 3072], P('dp', 'seq', 'tensor')
- grad_queries: bfloat16 [2, 4096, 3072], P('dp', 'seq', 'tensor')
- grad_keys: bfloat16 [2, 8192, 3072], P('dp', 'seq', 'tensor')
- grad_values: bfloat16 [2, 8192, 3072], P('dp', 'seq', 'tensor')
- grad_gain: float32 [3072], P('tensor')
Inputs may be any that keep to these rules, and one draw needn't show every extreme that they name: Along the token blocks of a recording band_start and band_end never fall and band_start < band_end; the band of a token block held by seq index j lies within encoder blocks (j - 2) * (2) to (j + 3) * 2 - 1, and in every draw some bands reach both of these limits.
All inputs are finite; a program needn't handle non-finite values.
Results may differ from a plain program's by a relative error of at most 0.008.
Values may be sent and summed in bfloat16 or wider, within the bound.
No kernel may reach another device: no remote copies, remote signals or barrier semaphores. Data moves between devices by JAX's collectives and lax.ppermute only.
A program may use at most 64 MiB of HBM per device.

v0:
```python
import jax
import jax.numpy as jnp
from jax import lax
from jax.sharding import PartitionSpec as P

D = 3072
HD = 96
TB = 128
EB = 128
REACH = 2


epsilon = 1e-06


def shifted(array, axis, by):
    size = lax.axis_size(axis)
    pairs = [(i, i + by) for i in range(size) if 0 <= i + by < size]
    return lax.ppermute(array, axis, pairs)


def head_probs(query_head, key_head, allowed, scale):
    scores = (
        lax.dot_general(
            query_head, key_head, (((1,), (1,)), ((), ())), preferred_element_type=jnp.float32
        )
        * scale
    )
    scores = jnp.where(allowed, scores, -jnp.inf)
    top = jnp.max(scores, axis=1, keepdims=True)
    weights = jnp.exp(scores - top)
    return weights / jnp.sum(weights, axis=1, keepdims=True)


def per_device(queries, keys, values, grad_out, gain, band_start, band_end):
    query_local = queries[0]
    key_local = keys[0]
    value_local = values[0]
    grad_local = grad_out[0].astype(jnp.float32)
    starts = band_start[0]
    ends = band_end[0]
    tok_rows, width = query_local.shape
    frame_rows = key_local.shape[0]
    heads = width // HD
    scale = HD ** (-0.5)
    here = lax.axis_index("seq")
    pair = jnp.stack([key_local, value_local])
    pieces = []
    for offset in range(-REACH, REACH + 1):
        if offset == 0:
            pieces.append(pair)
        else:
            pieces.append(shifted(pair, "seq", -offset))
    window = jnp.concatenate(pieces, axis=1)
    key_window = window[0]
    value_window = window[1]
    span = key_window.shape[0]
    frame_block = ((here - REACH) * frame_rows + jnp.arange(span, dtype=jnp.int32)) // EB
    row_start = jnp.repeat(starts, TB)
    row_end = jnp.repeat(ends, TB)
    allowed = (frame_block[None, :] >= row_start[:, None]) & (
        frame_block[None, :] < row_end[:, None]
    )
    outputs = []
    kept_probs = []
    for head in range(heads):
        columns = slice(head * HD, (head + 1) * HD)
        probs = head_probs(query_local[:, columns], key_window[:, columns], allowed, scale)
        kept_probs.append(probs)
        outputs.append(
            jnp.dot(
                probs.astype(jnp.bfloat16),
                value_window[:, columns],
                preferred_element_type=jnp.float32,
            )
        )
    attn = jnp.concatenate(outputs, axis=1)
    scaled_grad = grad_local * gain[None, :]
    square_local = jnp.sum(attn * attn, axis=1)
    cross_local = jnp.sum(scaled_grad * attn, axis=1)
    square_total = lax.psum(square_local, "tensor")
    inv_rms = lax.rsqrt(square_total / D + epsilon)
    normed = attn * inv_rms[:, None]
    attended = (normed * gain[None, :]).astype(jnp.bfloat16)
    cross_total = lax.psum(cross_local, "tensor")
    mean_cross = inv_rms * cross_total / D
    grad_attn = (inv_rms[:, None] * (scaled_grad - normed * mean_cross[:, None])).astype(
        jnp.bfloat16
    )
    grad_gain = lax.psum(jnp.sum(grad_local * normed, axis=0), ("dp", "seq"))
    query_grads = []
    key_grads = []
    value_grads = []
    for head in range(heads):
        columns = slice(head * HD, (head + 1) * HD)
        query_head = query_local[:, columns]
        key_head = key_window[:, columns]
        value_head = value_window[:, columns]
        grad_head = grad_attn[:, columns]
        probs = kept_probs[head]
        probs_b = probs.astype(jnp.bfloat16)
        grad_probs = lax.dot_general(
            grad_head, value_head, (((1,), (1,)), ((), ())), preferred_element_type=jnp.float32
        )
        inner = jnp.sum(probs * grad_probs, axis=1, keepdims=True)
        grad_scores = (probs * (grad_probs - inner)).astype(jnp.bfloat16)
        query_grads.append(
            scale * jnp.dot(grad_scores, key_head, preferred_element_type=jnp.float32)
        )
        key_grads.append(
            scale
            * lax.dot_general(
                grad_scores,
                query_head,
                (((0,), (0,)), ((), ())),
                preferred_element_type=jnp.float32,
            )
        )
        value_grads.append(
            lax.dot_general(
                probs_b, grad_head, (((0,), (0,)), ((), ())), preferred_element_type=jnp.float32
            )
        )
    grad_queries = jnp.concatenate(query_grads, axis=1).astype(jnp.bfloat16)
    window_grads = jnp.stack(
        [jnp.concatenate(key_grads, axis=1), jnp.concatenate(value_grads, axis=1)]
    )
    parts = [
        window_grads[:, index * frame_rows : (index + 1) * frame_rows]
        for index in range(2 * REACH + 1)
    ]
    total = parts[REACH]
    for offset in range(-REACH, REACH + 1):
        if offset != 0:
            total = total + shifted(
                parts[REACH + offset].astype(jnp.bfloat16), "seq", offset
            ).astype(jnp.float32)
    grad_keys = total[0].astype(jnp.bfloat16)
    grad_values = total[1].astype(jnp.bfloat16)
    return (attended[None], grad_queries[None], grad_keys[None], grad_values[None], grad_gain)


def solution(mesh):
    return jax.shard_map(
        per_device,
        mesh=mesh,
        in_specs=(
            P("dp", "seq", "tensor"),
            P("dp", "seq", "tensor"),
            P("dp", "seq", "tensor"),
            P("dp", "seq", "tensor"),
            P("tensor"),
            P("dp", "seq"),
            P("dp", "seq"),
        ),
        out_specs=(
            P("dp", "seq", "tensor"),
            P("dp", "seq", "tensor"),
            P("dp", "seq", "tensor"),
            P("dp", "seq", "tensor"),
            P("tensor"),
        ),
        check_vma=False,
    )
```

profile of v0, /device:TPU:6, one launch (start us, length us, event | category | flops | bytes accessed | tf_op | source)
XLA Modules:
  0.0 224.1 jit_solution(527827791470561601)
XLA Ops:
  0.7 1.0 constant_dynamic-update-slice_fusion.1
  1.7 1.0 constant_dynamic-update-slice_fusion
  2.6 3.8 %collective-permute-start = (bf16[2,256,384]{2,1,0:T(8,128)(2,1)S(1)}, bf16[2,256,384]{2,1,0:T(8,128)(2,1)S(1)}, u32[]{:S(2)}, u32[]{:S(2)}) collective-permute-start(bf16[2,256,384]{2,1,0:T(8,128)(2,1)S(1)} %constant_dynamic-update-slice_fusion), channel_id=1, source_target_pairs={{0,16},{8,24},{16,32},{24,40},{32,48},{40,56},{48,64},{56,72},{64,... | collective-permute-start | bytes 1179656 | tf_op jit(solution)/shard_map/ppermute | solution.py:19
  6.5 1.5 collective-permute-start.1
  8.0 1.3 collective-permute-start.2
  9.3 1.3 collective-permute-start.3
  11.9 1.0 copy.12
  12.9 3.0 %collective-permute-done = bf16[2,256,384]{2,1,0:T(8,128)(2,1)S(1)} collective-permute-done((bf16[2,256,384]{2,1,0:T(8,128)(2,1)S(1)}, bf16[2,256,384]{2,1,0:T(8,128)(2,1)S(1)}, u32[]{:S(2)}, u32[]{:S(2)}) %collective-permute-start) | collective-permute-done | bytes 393248 | tf_op jit(solution)/shard_map/ppermute | solution.py:19
  16.2 11.9 %collective-permute-done.3 = bf16[2,256,384]{2,1,0:T(8,128)(2,1)S(1)} collective-permute-done((bf16[2,256,384]{2,1,0:T(8,128)(2,1)S(1)}, bf16[2,256,384]{2,1,0:T(8,128)(2,1)S(1)}, u32[]{:S(2)}, u32[]{:S(2)}) %collective-permute-start.3) | collective-permute-done | bytes 393248 | tf_op jit(solution)/shard_map/ppermute | solution.py:19
  33.1 20.7 %psum.21 = f32[128]{0:T(128)S(1)} all-reduce(f32[128]{0:T(128)S(1)} %multiply_reduce_fusion), channel_id=1, replica_groups=mesh['dp'=2,'seq'=32,'tensor'=8] {'tensor'}, use_global_device_ids=true, to_apply=%region_9.10 | all-reduce | flops 128 | bytes 1024 | tf_op jit(solution)/shard_map/psum | solution.py:81
  54.1 23.3 %psum.22 = f32[128]{0:T(128)S(1)} all-reduce(f32[128]{0:T(128)S(1)} %get-tuple-element.11), channel_id=1, replica_groups=mesh['dp'=2,'seq'=32,'tensor'=8] {'tensor'}, use_global_device_ids=true, to_apply=%region_11.12 | all-reduce | flops 128 | bytes 1024 | tf_op jit(solution)/shard_map/psum | solution.py:85
  77.5 1.4 fusion.19
  79.3 1.2 fusion.23
  80.5 1.1 fusion.25
  83.1 1.2 convolution_multiply_fusion.5
  84.3 1.1 fusion.70
  85.3 1.1 fusion.69
  86.4 1.0 fusion.68
  87.4 1.1 fusion.67
  88.6 0.8 copy.21
  89.4 1.2 fusion.24
  91.8 0.9 copy-done.11
  93.6 0.9 copy-done
  94.5 1.0 fusion.98
  95.6 3.8 %collective-permute-start.7 = (bf16[2,256,384]{1,2,0:T(8,128)(2,1)}, bf16[2,256,384]{1,2,0:T(8,128)(2,1)S(1)}, u32[]{:S(2)}, u32[]{:S(2)}) collective-permute-start(bf16[2,256,384]{1,2,0:T(8,128)(2,1)} %get-tuple-element.13), channel_id=1, source_target_pairs={{0,16},{8,24},{16,32},{24,40},{32,48},{40,56},{48,64},{56,72},{64,... | collective-permute-start | bytes 1179656 | tf_op jit(solution)/shard_map/ppermute | solution.py:19
  99.4 2.1 collective-permute-start.6
  101.5 1.3 collective-permute-start.5
  102.8 1.3 collective-permute-start.4
  105.6 115.3 %psum.23 = f32[384]{0:T(512)} all-reduce(f32[384]{0:T(512)S(1)} %get-tuple-element.10), channel_id=1, replica_groups=mesh['dp'=2,'seq'=32,'tensor'=8] {'dp','seq'}, use_global_device_ids=true, to_apply=%region_17.18 | all-reduce | flops 384 | bytes 3072 | tf_op jit(solution)/shard_map/psum | solution.py:90
  220.9 1.6 fusion.18
  222.5 0.8 copy.23
  223.3 0.8 copy.24
  (79 shorter events, 11.2 us)
Async XLA Ops:
  0.6 15.4 %copy-start.7 = (bf16[1,256,384]{2,1,0:T(8,128)(2,1)S(1)}, bf16[1,256,384]{2,1,0:T(8,128)(2,1)}, u32[]{:S(2)}) copy-start(bf16[1,256,384]{2,1,0:T(8,128)(2,1)} %param.8) | copy-start | bytes 589828
  0.6 15.5 %copy-start.8 = (bf16[1,256,384]{2,1,0:T(8,128)(2,1)S(1)}, bf16[1,256,384]{2,1,0:T(8,128)(2,1)}, u32[]{:S(2)}) copy-start(bf16[1,256,384]{2,1,0:T(8,128)(2,1)} %param.9) | copy-start | bytes 589828
  2.6 13.3 %collective-permute-start = (bf16[2,256,384]{2,1,0:T(8,128)(2,1)S(1)}, bf16[2,256,384]{2,1,0:T(8,128)(2,1)S(1)}, u32[]{:S(2)}, u32[]{:S(2)}) collective-permute-start(bf16[2,256,384]{2,1,0:T(8,128)(2,1)S(1)} %constant_dynamic-update-slice_fusion), channel_id=1, source_target_pairs={{0,16},{8,24},{16,32},{24,40},{32,48},{40,56},{48,64},{56,72},{64,... | collective-permute-start | bytes 1179656 | tf_op jit(solution)/shard_map/ppermute | solution.py:19
  6.5 9.5 %collective-permute-start.1 = (bf16[2,256,384]{2,1,0:T(8,128)(2,1)S(1)}, bf16[2,256,384]{2,1,0:T(8,128)(2,1)S(1)}, u32[]{:S(2)}, u32[]{:S(2)}) collective-permute-start(bf16[2,256,384]{2,1,0:T(8,128)(2,1)S(1)} %constant_dynamic-update-slice_fusion), channel_id=1, source_target_pairs={{0,8},{8,16},{16,24},{24,32},{32,40},{40,48},{48,56},{56,64},{64,7... | collective-permute-start | bytes 1179656 | tf_op jit(solution)/shard_map/ppermute | solution.py:19
  8.0 8.2 %collective-permute-start.2 = (bf16[2,256,384]{2,1,0:T(8,128)(2,1)S(1)}, bf16[2,256,384]{2,1,0:T(8,128)(2,1)S(1)}, u32[]{:S(2)}, u32[]{:S(2)}) collective-permute-start(bf16[2,256,384]{2,1,0:T(8,128)(2,1)S(1)} %constant_dynamic-update-slice_fusion), channel_id=1, source_target_pairs={{8,0},{16,8},{24,16},{32,24},{40,32},{48,40},{56,48},{64,56},{72,6... | collective-permute-start | bytes 1179656 | tf_op jit(solution)/shard_map/ppermute | solution.py:19
  9.3 18.8 %collective-permute-start.3 = (bf16[2,256,384]{2,1,0:T(8,128)(2,1)S(1)}, bf16[2,256,384]{2,1,0:T(8,128)(2,1)S(1)}, u32[]{:S(2)}, u32[]{:S(2)}) collective-permute-start(bf16[2,256,384]{2,1,0:T(8,128)(2,1)S(1)} %constant_dynamic-update-slice_fusion), channel_id=1, source_target_pairs={{16,0},{24,8},{32,16},{40,24},{48,32},{56,40},{64,48},{72,56},{80,... | collective-permute-start | bytes 1179656 | tf_op jit(solution)/shard_map/ppermute | solution.py:19
  28.2 0.9 copy-start.9
  28.4 2.3 %copy-start.1 = (bf16[1280,384]{1,0:T(8,128)(2,1)}, bf16[1280,384]{1,0:T(8,128)(2,1)S(1)}, u32[]{:S(2)}) copy-start(bf16[1280,384]{1,0:T(8,128)(2,1)S(1)} %get-tuple-element.16) | copy-start | bytes 2949124
  28.4 4.3 %copy-start.5 = (bf16[1280,384]{1,0:T(8,128)(2,1)}, bf16[1280,384]{1,0:T(8,128)(2,1)S(1)}, u32[]{:S(2)}) copy-start(bf16[1280,384]{1,0:T(8,128)(2,1)S(1)} %get-tuple-element.17) | copy-start | bytes 2949124
  32.5 21.3 %copy-start.15 = (f32[384]{0:T(512)S(1)}, f32[384]{0:T(512)}, u32[]{:S(2)}) copy-start(f32[384]{0:T(512)} %param.11) | copy-start | bytes 4612
  77.3 1.6 copy-start.6
  80.5 1.3 copy-start.2
  88.5 2.5 %copy-start.10 = (f32[128,1280]{0,1:T(8,128)S(1)}, f32[128,1280]{0,1:T(8,128)}, u32[]{:S(2)}) copy-start(f32[128,1280]{0,1:T(8,128)} %get-tuple-element.35) | copy-start | bytes 1966084
  90.6 1.0 copy-start.4
  91.6 1.0 copy-start.11
  91.6 1.2 copy-start.12
  91.6 1.3 copy-start.13
  91.6 1.5 copy-start.14
  93.2 1.3 copy-start
  94.5 9.5 %copy-start.3 = (bf16[1280,384]{1,0:T(8,128)(2,1)S(1)}, bf16[1280,384]{1,0:T(8,128)(2,1)}, u32[]{:S(2)}) copy-start(bf16[1280,384]{1,0:T(8,128)(2,1)} %copy-done.1) | copy-start | bytes 2949124
  95.6 125.3 %collective-permute-start.7 = (bf16[2,256,384]{1,2,0:T(8,128)(2,1)}, bf16[2,256,384]{1,2,0:T(8,128)(2,1)S(1)}, u32[]{:S(2)}, u32[]{:S(2)}) collective-permute-start(bf16[2,256,384]{1,2,0:T(8,128)(2,1)} %get-tuple-element.13), channel_id=1, source_target_pairs={{0,16},{8,24},{16,32},{24,40},{32,48},{40,56},{48,64},{56,72},{64,... | collective-permute-start | bytes 1179656 | tf_op jit(solution)/shard_map/ppermute | solution.py:19
  99.4 121.4 %collective-permute-start.6 = (bf16[2,256,384]{1,2,0:T(8,128)(2,1)}, bf16[2,256,384]{1,2,0:T(8,128)(2,1)}, u32[]{:S(2)}, u32[]{:S(2)}) collective-permute-start(bf16[2,256,384]{1,2,0:T(8,128)(2,1)} %get-tuple-element.14), channel_id=1, source_target_pairs={{0,8},{8,16},{16,24},{24,32},{32,40},{40,48},{48,56},{56,64},{64,7... | collective-permute-start | bytes 1179656 | tf_op jit(solution)/shard_map/ppermute | solution.py:19
  101.5 119.4 %collective-permute-start.5 = (bf16[2,256,384]{1,2,0:T(8,128)(2,1)}, bf16[2,256,384]{1,2,0:T(8,128)(2,1)}, u32[]{:S(2)}, u32[]{:S(2)}) collective-permute-start(bf16[2,256,384]{1,2,0:T(8,128)(2,1)} %get-tuple-element.15), channel_id=1, source_target_pairs={{8,0},{16,8},{24,16},{32,24},{40,32},{48,40},{56,48},{64,56},{72,6... | collective-permute-start | bytes 1179656 | tf_op jit(solution)/shard_map/ppermute | solution.py:19
  102.8 118.1 %collective-permute-start.4 = (bf16[2,256,384]{1,2,0:T(8,128)(2,1)S(1)}, bf16[2,256,384]{1,2,0:T(8,128)(2,1)}, u32[]{:S(2)}, u32[]{:S(2)}) collective-permute-start(bf16[2,256,384]{1,2,0:T(8,128)(2,1)S(1)} %get-tuple-element.12), channel_id=1, source_target_pairs={{16,0},{24,8},{32,16},{40,24},{48,32},{56,40},{64,48},{72,56},{80,... | collective-permute-start | bytes 1179656 | tf_op jit(solution)/shard_map/ppermute | solution.py:19
where the time goes:
time: 225 us; the launch traced here: 224 us
  blocking collectives  159 us (71%)
  starting transfers between devices  16.4 us (7%)
  matrix products  15.2 us (7%)
  waiting for transfers between devices  14.9 us (7%)
  local copies, waits for them, and re-layouts  10.8 us (5%)
  other arithmetic  5.26 us (2%)
  between operations  2.34 us (1%)
    psum x1, blocking collectives, per_device(): grad_gain = lax.psum(jnp.sum(grad_local * normed, axis=0), ('dp', 'seq'))  115 us
    psum x1, blocking collectives, per_device(): cross_total = lax.psum(cross_local, 'tensor')  23.3 us
    psum x1, blocking collectives, per_device(): square_total = lax.psum(square_local, 'tensor')  20.7 us
    ppermute x8, starting transfers between devices, shifted(): return lax.ppermute(array, axis, pairs)  16.4 us
    ppermute x8, waiting for transfers between devices, shifted(): return lax.ppermute(array, axis, pairs)  14.9 us
    unnamed x43, local copies, waits for them, and re-layouts  8.52 us
  transfers between devices with their start and end apart: 8, of which 2 were waited for; matrix products, arithmetic and copies ran while one was open for 1% of the time, Pallas kernels for 0%

commit v1 on v0

v1 whole, which is shorter than its diff:
```python
import jax
import jax.numpy as jnp
from jax import lax
from jax.experimental import pallas as pl
from jax.experimental.pallas import tpu as pltpu
from jax.sharding import PartitionSpec as P

D = 3072
HD = 96
TB = 128
EB = 128
FR = 256
W = 384
TENSOR = 8
SEQ = 32
SCALE = HD ** (-0.5)
epsilon = 1e-06

PIECES = 5
NT = (((1,), (1,)), ((), ()))
TN = (((0,), (0,)), ((), ()))
PAIRS = ((0, (0, 96)), (128, (64, 160)))


def permute(array, axis, target):
    size = lax.axis_size(axis)
    pairs = [(i, target(i)) for i in range(size) if 0 <= target(i) < size]
    return lax.ppermute(array, axis, pairs)


def offsets(here):
    core = lax.rem(here, 2)
    toward = 1 - 2 * core
    return (0, toward, -2, 2, -toward)


def blocked(rows, pair):
    first, starts = PAIRS[pair]
    part = rows[:, first : first + 256]
    lane = lax.broadcasted_iota(jnp.int32, part.shape, 1)
    zero = jnp.zeros_like(part)
    return jnp.concatenate(
        [jnp.where((lane >= at) & (lane < at + HD), part, zero) for at in starts], axis=0
    )


def side_by_side(pairs):
    lane = lax.broadcasted_iota(jnp.int32, (TB, 256), 1)
    low = jnp.where(lane < HD, pairs[0][:TB], pairs[0][TB:])
    high = jnp.where(lane < 160, pairs[1][:TB], pairs[1][TB:])
    middle = jnp.where(lane[:, :128] < 64, low[:, 128:], high[:, :128])
    return jnp.concatenate([low[:, :128], middle, high[:, 128:]], axis=1)


def to_rows(columns):
    lane = lax.broadcasted_iota(jnp.int32, (TB, TB), 1)
    tile = jnp.zeros((TB, TB), jnp.float32)
    for index, column in enumerate(columns):
        tile = jnp.where(lane == index, column, tile)
    return tile.T


def forward_kernel(
    start_ref, end_ref, q_ref, go_ref, gain_ref, *rest
):
    pieces = rest[:PIECES]
    attn_ref, probs_ref, stats_ref, scores = rest[PIECES:]
    here = lax.axis_index("seq")
    first = start_ref[0, 0]
    last = end_ref[0, 0]
    rows = q_ref[...]
    results = []
    for pair in range(2):
        at = PAIRS[pair][0]
        block = blocked(rows, pair)
        top = None
        for index, offset in enumerate(offsets(here)):
            frames = 2 * (here + offset)
            product = (
                lax.dot_general(
                    block,
                    pieces[index][0:FR, at : at + 256],
                    NT,
                    preferred_element_type=jnp.float32,
                )
                * SCALE
            )
            for half in range(2):
                allowed = (frames + half >= first) & (frames + half < last)
                bias = jnp.where(allowed, 0.0, -jnp.inf)
                part = product[:, half * EB : (half + 1) * EB] + bias
                scores[pair, :, index * FR + half * EB : index * FR + (half + 1) * EB] = part
                top = part if top is None else jnp.maximum(top, part)
        top = jnp.max(top, axis=1, keepdims=True)
        weights = jnp.exp(scores[pair] - top)
        total = jnp.sum(weights, axis=1, keepdims=True)
        probs = weights * (1.0 / total)
        probs_ref[pair] = probs
        probs = probs.astype(jnp.bfloat16)
        acc = None
        for index in range(PIECES):
            part = jnp.dot(
                probs[:, index * FR : (index + 1) * FR],
                pieces[index][FR : 2 * FR, at : at + 256],
                preferred_element_type=jnp.float32,
            )
            acc = part if acc is None else acc + part
        results.append(acc)
    attn = side_by_side(results)
    attn_ref[...] = attn
    scaled = go_ref[...].astype(jnp.float32) * gain_ref[...]
    square = jnp.sum(attn * attn, axis=1, keepdims=True)
    cross = jnp.sum(scaled * attn, axis=1, keepdims=True)
    stats = to_rows([square, cross])[0:2]
    for index in range(TENSOR):
        stats_ref[index] = stats


def backward_kernel(q_ref, go_ref, gain_ref, attn_ref, probs_ref, stats_ref, *rest):
    pieces = rest[:PIECES]
    attended_ref, gain_part_ref, gq_ref, own_ref = rest[PIECES : PIECES + 4]
    outs = rest[PIECES + 4 : PIECES + 8]
    grads = rest[PIECES + 8]
    stats = stats_ref[0]
    for index in range(1, TENSOR):
        stats = stats + stats_ref[index]
    row = lax.broadcasted_iota(jnp.int32, (TB, TB), 0)
    tile = jnp.where(row == 0, stats[0:1], jnp.where(row == 1, stats[1:2], 0.0)).T
    inv = lax.rsqrt(tile[:, 0:1] / D + epsilon)
    mean_cross = inv * tile[:, 1:2] / D
    grad = go_ref[...].astype(jnp.float32)
    gain = gain_ref[...]
    normed = attn_ref[...] * inv
    attended_ref[...] = (normed * gain).astype(jnp.bfloat16)
    gain_part_ref[...] = jnp.sum(grad * normed, axis=0, keepdims=True)
    grad_attn = (inv * (grad * gain - normed * mean_cross)).astype(jnp.bfloat16)
    rows = q_ref[...]
    grad_q = []
    grad_kv = [[None, None] for _ in range(PIECES)]
    for pair in range(2):
        at = PAIRS[pair][0]
        block = blocked(rows, pair)
        cot = blocked(grad_attn, pair)
        inner = None
        for index in range(PIECES):
            part = lax.dot_general(
                cot,
                pieces[index][FR : 2 * FR, at : at + 256],
                NT,
                preferred_element_type=jnp.float32,
            )
            grads[:, index * FR : (index + 1) * FR] = part
            part = probs_ref[pair, :, index * FR : (index + 1) * FR] * part
            inner = part if inner is None else inner + part
        inner = jnp.sum(inner, axis=1, keepdims=True)
        acc = None
        for index in range(PIECES):
            span = slice(index * FR, (index + 1) * FR)
            probs = probs_ref[pair, :, span]
            ds = (probs * (grads[:, span] - inner)).astype(jnp.bfloat16)
            part = jnp.dot(
                ds, pieces[index][0:FR, at : at + 256], preferred_element_type=jnp.float32
            )
            acc = part if acc is None else acc + part
            gk = lax.dot_general(ds, block, TN, preferred_element_type=jnp.float32) * SCALE
            gv = lax.dot_general(
                probs.astype(jnp.bfloat16), cot, TN, preferred_element_type=jnp.float32
            )
            out = own_ref if index == 0 else outs[index - 1]
            for base, value in ((0, gk), (FR, gv)):
                span_rows = slice(base, base + FR)
                if pair == 0:
                    out[span_rows, 0:128] = value[:, 0:128].astype(out.dtype)
                    grad_kv[index][base // FR] = value[:, 128:256]
                else:
                    middle = grad_kv[index][base // FR] + value[:, 0:128]
                    out[span_rows, 128:256] = middle.astype(out.dtype)
                    out[span_rows, 256:384] = value[:, 128:256].astype(out.dtype)
        grad_q.append(acc)
    gq_ref[...] = (side_by_side(grad_q) * SCALE).astype(jnp.bfloat16)


VMEM = pl.BlockSpec(memory_space=pltpu.VMEM)
SMEM = pl.BlockSpec(memory_space=pltpu.SMEM)


def per_device(queries, keys, values, grad_out, gain, band_start, band_end):
    f32, bf16 = jnp.float32, jnp.bfloat16
    here = lax.axis_index("seq")
    core = lax.rem(here, 2)
    own = jnp.concatenate([keys[0], values[0]], axis=0)
    below = permute(own, "seq", lambda i: i + 2)
    above = permute(own, "seq", lambda i: i - 2)
    partner = permute(own, "seq", lambda i: i ^ 1)
    beyond = permute(jnp.where(core == 0, above, below), "seq", lambda i: i ^ 1)
    pieces = (own, partner, below, above, beyond)
    query = queries[0]
    grad = grad_out[0]
    gain_row = gain[None]
    attn, probs, stats = pl.pallas_call(
        forward_kernel,
        out_shape=(
            jax.ShapeDtypeStruct((TB, W), f32),
            jax.ShapeDtypeStruct((2, 2 * TB, PIECES * FR), f32),
            jax.ShapeDtypeStruct((TENSOR, 2, TB), f32),
        ),
        in_specs=[SMEM, SMEM] + [VMEM] * (3 + PIECES),
        out_specs=(VMEM, VMEM, VMEM),
        scratch_shapes=[pltpu.VMEM((2, 2 * TB, PIECES * FR), f32)],
        name="attention_forward",
    )(band_start, band_end, query, grad, gain_row, *pieces)
    stats = lax.all_to_all(stats, "tensor", 0, 0, tiled=False)
    back = pl.pallas_call(
        backward_kernel,
        out_shape=(
            jax.ShapeDtypeStruct((TB, W), bf16),
            jax.ShapeDtypeStruct((1, W), f32),
            jax.ShapeDtypeStruct((TB, W), bf16),
            jax.ShapeDtypeStruct((2 * FR, W), f32),
        )
        + (jax.ShapeDtypeStruct((2 * FR, W), bf16),) * 4,
        in_specs=[VMEM] * (6 + PIECES),
        out_specs=(VMEM,) * 8,
        scratch_shapes=[pltpu.VMEM((2 * TB, PIECES * FR), f32)],
        name="attention_backward",
    )(query, grad, gain_row, attn, probs, stats, *pieces)
    attended, gain_part, grad_queries, total, to_partner, to_below, to_above, to_beyond = back
    got = [
        permute(to_below, "seq", lambda i: i - 2),
        permute(to_above, "seq", lambda i: i + 2),
        permute(to_beyond, "seq", lambda i: i - 1 if i % 2 == 0 else i + 1),
        permute(to_partner, "seq", lambda i: i ^ 1),
    ]
    gain_pair = gain_part + lax.ppermute(gain_part, "dp", [(0, 1), (1, 0)])
    spread = lax.all_to_all(
        jnp.broadcast_to(gain_pair, (SEQ, W)), "seq", 0, 0, tiled=True
    )
    grad_gain = jnp.sum(spread, axis=0)
    for part in got:
        total = total + part.astype(f32)
    total = total.astype(bf16)
    return (
        attended[None],
        grad_queries[None],
        total[None, :FR],
        total[None, FR:],
        grad_gain,
    )


def solution(mesh):
    return jax.shard_map(
        per_device,
        mesh=mesh,
        in_specs=(
            P("dp", "seq", "tensor"),
            P("dp", "seq", "tensor"),
            P("dp", "seq", "tensor"),
            P("dp", "seq", "tensor"),
            P("tensor"),
            P("dp", "seq"),
            P("dp", "seq"),
        ),
        out_specs=(
            P("dp", "seq", "tensor"),
            P("dp", "seq", "tensor"),
            P("dp", "seq", "tensor"),
            P("dp", "seq", "tensor"),
            P("tensor"),
        ),
        check_vma=False,
    )
```

time: 225 us -> 98.1 us (0.44)
  the two profiles are of different devices: /device:TPU:6 before, /device:TPU:1 now
where the time goes in v1:
time: 98.1 us; the launch traced here: 97.6 us
  blocking collectives  40.9 us (42%)
  starting transfers between devices  35 us (36%)
  Pallas kernels  10.4 us (11%)
  other arithmetic  3.81 us (4%)
  local copies, waits for them, and re-layouts  2.93 us (3%)
  waiting for transfers between devices  2.32 us (2%)
  between operations  2.11 us (2%)
    ppermute x8, starting transfers between devices, permute(): return lax.ppermute(array, axis, pairs)  32.8 us
    all_to_all x1, blocking collectives, per_device(): lax.all_to_all(jnp.broadcast_to(gain_pair, (SEQ, W)), 'seq', 0, 0, tiled=...  30 us
    all_to_all x1, blocking collectives, per_device(): stats = lax.all_to_all(stats, 'tensor', 0, 0, tiled=False)  10.9 us
    pallas_call x1, Pallas kernels, per_device(): pl.pallas_call(backward_kernel, out_shape=(jax.ShapeDtypeStruct((TB, W),...  5.87 us
    pallas_call x1, Pallas kernels, per_device(): pl.pallas_call(forward_kernel, out_shape=(jax.ShapeDtypeStruct((TB, W), f...  4.54 us
    ppermute x1, waiting for transfers between devices, per_device(): gain_pair = gain_part + lax.ppermute(gain_part, 'dp', [(0, 1), (1, 0)])  2.3 us
    ppermute x1, starting transfers between devices, per_device(): gain_pair = gain_part + lax.ppermute(gain_part, 'dp', [(0, 1), (1, 0)])  2.22 us
  transfers between devices with their start and end apart: 9, of which 1 were waited for; matrix products, arithmetic and copies ran while one was open for 3% of the time, Pallas kernels for 0%

profile of v1, /device:TPU:1, one launch (start us, length us, event | category | flops | bytes accessed | tf_op | source)
XLA Modules:
  0.0 97.6 jit_solution(12421070884659423357)
XLA Ops:
  0.6 1.1 %pad_maximum_fusion.rest_0_ = bf16[512,384]{1,0:T(8,128)(2,1)S(1)} fusion(bf16[256,384]{1,0:T(8,128)(2,1)} %bitcast.14, bf16[256,384]{1,0:T(8,128)(2,1)} %bitcast.15), kind=kLoop, calls=%fused_computation.1 | loop fusion | flops 786432 | bytes 786432 | tf_op jit(solution)/shard_map/concatenate | solution.py:191
  1.7 1.3 %collective-permute-start.2 = (bf16[512,384]{1,0:T(8,128)(2,1)S(1)}, bf16[512,384]{1,0:T(8,128)(2,1)S(1)}, u32[]{:S(2)}, u32[]{:S(2)}) collective-permute-start(bf16[512,384]{1,0:T(8,128)(2,1)S(1)} %pad_maximum_fusion.rest_0_), channel_id=1, source_target_pairs={{16,0},{24,8},{32,16},{40,24},{48,32},{56,40},{64,48},{72,56},{80,... | collective-permute-start | bytes 1179656 | tf_op jit(solution)/shard_map/ppermute | solution.py:28
  3.0 5.0 %collective-permute-start.1 = (bf16[512,384]{1,0:T(8,128)(2,1)S(1)}, bf16[512,384]{1,0:T(8,128)(2,1)S(1)}, u32[]{:S(2)}, u32[]{:S(2)}) collective-permute-start(bf16[512,384]{1,0:T(8,128)(2,1)S(1)} %pad_maximum_fusion.rest_0_), channel_id=1, source_target_pairs={{0,16},{8,24},{16,32},{24,40},{32,48},{40,56},{48,64},{56,72},{64,... | collective-permute-start | bytes 1179656 | tf_op jit(solution)/shard_map/ppermute | solution.py:28
  8.0 8.3 %collective-permute-start = (bf16[512,384]{1,0:T(8,128)(2,1)S(1)}, bf16[512,384]{1,0:T(8,128)(2,1)S(1)}, u32[]{:S(2)}, u32[]{:S(2)}) collective-permute-start(bf16[512,384]{1,0:T(8,128)(2,1)S(1)} %pad_maximum_fusion.rest_0_), channel_id=1, source_target_pairs={{0,8},{8,0},{16,24},{24,16},{32,40},{40,32},{48,56},{56,48},{64,72... | collective-permute-start | bytes 1179656 | tf_op jit(solution)/shard_map/ppermute | solution.py:28
  16.3 0.0 collective-permute-done.2.rest_3_
  16.4 0.0 collective-permute-done.1.rest_2_
  16.4 0.0 copy-start.2
  16.4 0.1 broadcast_select_fusion
  16.4 5.2 %collective-permute-start.3 = (bf16[512,384]{1,0:T(8,128)(2,1)S(1)}, bf16[512,384]{1,0:T(8,128)(2,1)S(1)}, u32[]{:S(2)}, u32[]{:S(2)}) collective-permute-start(bf16[512,384]{1,0:T(8,128)(2,1)S(1)} %broadcast_select_fusion), channel_id=1, source_target_pairs={{0,8},{8,0},{16,24},{24,16},{32,40},{40,32},{48,56},{56,48},{64,72... | collective-permute-start | bytes 1179656 | tf_op jit(solution)/shard_map/ppermute | solution.py:28
  22.9 1.2 %broadcast_in_dim.20.gain_ref = f32[1,384]{1,0:T(1,128)} reshape(f32[384]{0:T(512)} %param.11) | data formatting | bytes 3072 | tf_op jit(solution)/shard_map/broadcast_in_dim | solution.py:199
  24.2 0.0 collective-permute-done.rest_1_
  24.2 0.0 collective-permute-done.3.rest_4_
  24.2 0.7 copy-done.3
  25.0 0.1 copy-done.4
  25.1 4.5 %attention_forward.1 = (f32[128,384]{1,0:T(8,128)}, f32[2,256,1280]{2,1,0:T(8,128)}, f32[8,2,128]{2,1,0:T(2,128)}) custom-call(s32[1,1]{1,0:T(1,128)S(6)} %copy.14.start_ref, s32[1,1]{1,0:T(1,128)S(6)} %copy.15.end_ref, bf16[128,384]{1,0:T(8,128)(2,1)} %bitcast.10, bf16[128,384]{1,0:T(8,128)(2,1)} %bitcast.12, f32[1,384]{1,0:T(1,128)} %broadcast_in_dim.20.gain_ref, ...), custom_call_target="tpu_custom_call" | custom-call | tf_op jit(solution)/shard_map/attention_forward/pallas_call | solution.py:200
  29.6 10.9 %all_to_all.11.stats_ref = f32[8,2,128]{2,1,0:T(2,128)} all-to-all(f32[8,2,128]{2,1,0:T(2,128)} %get-tuple-element.18), channel_id=1, replica_groups=mesh['dp'=2,'seq'=32,'tensor'=8] {'tensor'}, dimensions={0} | all-to-all | bytes 16384 | tf_op jit(solution)/shard_map/all_to_all | solution.py:212
  40.6 5.9 %attention_backward.1 = (bf16[128,384]{1,0:T(8,128)(2,1)}, f32[1,384]{1,0:T(1,128)}, bf16[128,384]{1,0:T(8,128)(2,1)}, f32[512,384]{1,0:T(8,128)}, bf16[512,384]...) custom-call(bf16[128,384]{1,0:T(8,128)(2,1)} %bitcast.11, ...), custom_call_target="tpu_custom_call" | custom-call | tf_op jit(solution)/shard_map/attention_backward/pallas_call | solution.py:213
  46.4 1.3 %collective-permute-start.4 = (bf16[512,384]{1,0:T(8,128)(2,1)}, bf16[512,384]{1,0:T(8,128)(2,1)S(1)}, u32[]{:S(2)}, u32[]{:S(2)}) collective-permute-start(bf16[512,384]{1,0:T(8,128)(2,1)} %get-tuple-element.22), channel_id=1, source_target_pairs={{16,0},{24,8},{32,16},{40,24},{48,32},{56,40},{64,48},{72,56},{80,... | collective-permute-start | bytes 1179656 | tf_op jit(solution)/shard_map/ppermute | solution.py:28
  47.7 4.7 %collective-permute-start.5 = (bf16[512,384]{1,0:T(8,128)(2,1)}, bf16[512,384]{1,0:T(8,128)(2,1)S(1)}, u32[]{:S(2)}, u32[]{:S(2)}) collective-permute-start(bf16[512,384]{1,0:T(8,128)(2,1)} %get-tuple-element.23), channel_id=1, source_target_pairs={{0,16},{8,24},{16,32},{24,40},{32,48},{40,56},{48,64},{56,72},{64,... | collective-permute-start | bytes 1179656 | tf_op jit(solution)/shard_map/ppermute | solution.py:28
  52.5 5.1 %collective-permute-start.6 = (bf16[512,384]{1,0:T(8,128)(2,1)}, bf16[512,384]{1,0:T(8,128)(2,1)S(1)}, u32[]{:S(2)}, u32[]{:S(2)}) collective-permute-start(bf16[512,384]{1,0:T(8,128)(2,1)} %get-tuple-element.24), channel_id=1, source_target_pairs={{8,16},{16,8},{24,32},{32,24},{40,48},{48,40},{56,64},{64,56},{72,... | collective-permute-start | bytes 1179656 | tf_op jit(solution)/shard_map/ppermute | solution.py:28
  57.6 1.9 %collective-permute-start.7 = (bf16[512,384]{1,0:T(8,128)(2,1)}, bf16[512,384]{1,0:T(8,128)(2,1)S(1)}, u32[]{:S(2)}, u32[]{:S(2)}) collective-permute-start(bf16[512,384]{1,0:T(8,128)(2,1)} %get-tuple-element.25), channel_id=1, source_target_pairs={{0,8},{8,0},{16,24},{24,16},{32,40},{40,32},{48,56},{56,48},{64,72... | collective-permute-start | bytes 1179656 | tf_op jit(solution)/shard_map/ppermute | solution.py:28
  59.5 2.2 %collective-permute-start.8 = (f32[1,384]{1,0:T(1,128)}, f32[1,384]{1,0:T(1,128)S(1)}, u32[]{:S(2)}, u32[]{:S(2)}) collective-permute-start(f32[1,384]{1,0:T(1,128)} %get-tuple-element.26), channel_id=1, source_target_pairs={{0,256},{256,0},{1,257},{257,1},{2,258},{258,2},{3,259},{259,3},{4... | collective-permute-start | bytes 4616 | tf_op jit(solution)/shard_map/ppermute | solution.py:234
  61.7 2.3 %collective-permute-done.8 = f32[1,384]{1,0:T(1,128)S(1)} collective-permute-done((f32[1,384]{1,0:T(1,128)}, f32[1,384]{1,0:T(1,128)S(1)}, u32[]{:S(2)}, u32[]{:S(2)}) %collective-permute-start.8) | collective-permute-done | bytes 1568 | tf_op jit(solution)/shard_map/ppermute | solution.py:234
  64.0 0.7 add_reduce_fusion
  64.8 30.0 %all_to_all.12 = f32[32,1,384]{2,1,0:T(1,128)S(1)} all-to-all(f32[32,1,384]{2,1,0:T(1,128)S(1)} %broadcast_in_dim.25), channel_id=1, replica_groups=mesh['dp'=2,'seq'=32,'tensor'=8] {'seq'}, dimensions={0} | all-to-all | bytes 98304 | tf_op jit(solution)/shard_map/all_to_all | solution.py:235
  94.8 0.6 reduce_sum.9
  95.4 0.0 collective-permute-done.4
  95.4 0.0 collective-permute-done.5
  95.4 0.0 collective-permute-done.6
  95.4 0.0 collective-permute-done.7
  95.4 1.4 %add_convert_fusion = bf16[512,384]{1,0:T(8,128)(2,1)S(1)} fusion(bf16[512,384]{1,0:T(8,128)(2,1)S(1)} %collective-permute-done.7, bf16[512,384]{1,0:T(8,128)(2,1)S(1)} %collective-permute-done.6, bf16[512,384]{1,0:T(8,128)(2,1)S(1)} %collective-permute-done.5, f32[512,384]{1,0:T(8,128)} %get-tuple-element.21, bf16[512,384]{1,0:T(8,128)(2,1)S(1)} %collective-permute-done.4), kind=kLoop, calls=%fused_computation | loop fusion | flops 1769472 | bytes 2752512 | tf_op jit(solution)/shard_map/convert_element_type | solution.py:241
  96.8 0.8 slice_bitcast_fusion
  (8 shorter events, 0.0 us)
Async XLA Ops:
  1.7 22.5 %copy-start = (bf16[512,384]{1,0:T(8,128)(2,1)}, bf16[512,384]{1,0:T(8,128)(2,1)S(1)}, u32[]{:S(2)}) copy-start(bf16[512,384]{1,0:T(8,128)(2,1)S(1)} %pad_maximum_fusion.rest_0_) | copy-start | bytes 1179652
  1.7 14.6 %collective-permute-start.2 = (bf16[512,384]{1,0:T(8,128)(2,1)S(1)}, bf16[512,384]{1,0:T(8,128)(2,1)S(1)}, u32[]{:S(2)}, u32[]{:S(2)}) collective-permute-start(bf16[512,384]{1,0:T(8,128)(2,1)S(1)} %pad_maximum_fusion.rest_0_), channel_id=1, source_target_pairs={{16,0},{24,8},{32,16},{40,24},{48,32},{56,40},{64,48},{72,56},{80,... | collective-permute-start | bytes 1179656 | tf_op jit(solution)/shard_map/ppermute | solution.py:28
  3.0 13.4 %collective-permute-start.1 = (bf16[512,384]{1,0:T(8,128)(2,1)S(1)}, bf16[512,384]{1,0:T(8,128)(2,1)S(1)}, u32[]{:S(2)}, u32[]{:S(2)}) collective-permute-start(bf16[512,384]{1,0:T(8,128)(2,1)S(1)} %pad_maximum_fusion.rest_0_), channel_id=1, source_target_pairs={{0,16},{8,24},{16,32},{24,40},{32,48},{40,56},{48,64},{56,72},{64,... | collective-permute-start | bytes 1179656 | tf_op jit(solution)/shard_map/ppermute | solution.py:28
  8.0 16.2 %collective-permute-start = (bf16[512,384]{1,0:T(8,128)(2,1)S(1)}, bf16[512,384]{1,0:T(8,128)(2,1)S(1)}, u32[]{:S(2)}, u32[]{:S(2)}) collective-permute-start(bf16[512,384]{1,0:T(8,128)(2,1)S(1)} %pad_maximum_fusion.rest_0_), channel_id=1, source_target_pairs={{0,8},{8,0},{16,24},{24,16},{32,40},{40,32},{48,56},{56,48},{64,72... | collective-permute-start | bytes 1179656 | tf_op jit(solution)/shard_map/ppermute | solution.py:28
  16.4 7.9 %copy-start.1 = (bf16[512,384]{1,0:T(8,128)(2,1)}, bf16[512,384]{1,0:T(8,128)(2,1)S(1)}, u32[]{:S(2)}) copy-start(bf16[512,384]{1,0:T(8,128)(2,1)S(1)} %collective-permute-done.2.rest_3_) | copy-start | bytes 1179652
  16.4 7.9 %copy-start.2 = (bf16[512,384]{1,0:T(8,128)(2,1)}, bf16[512,384]{1,0:T(8,128)(2,1)S(1)}, u32[]{:S(2)}) copy-start(bf16[512,384]{1,0:T(8,128)(2,1)S(1)} %collective-permute-done.1.rest_2_) | copy-start | bytes 1179652
  16.4 7.8 %collective-permute-start.3 = (bf16[512,384]{1,0:T(8,128)(2,1)S(1)}, bf16[512,384]{1,0:T(8,128)(2,1)S(1)}, u32[]{:S(2)}, u32[]{:S(2)}) collective-permute-start(bf16[512,384]{1,0:T(8,128)(2,1)S(1)} %broadcast_select_fusion), channel_id=1, source_target_pairs={{0,8},{8,0},{16,24},{24,16},{32,40},{40,32},{48,56},{56,48},{64,72... | collective-permute-start | bytes 1179656 | tf_op jit(solution)/shard_map/ppermute | solution.py:28
  24.2 0.8 copy-start.3
  24.2 0.9 copy-start.4
  46.4 49.0 %collective-permute-start.4 = (bf16[512,384]{1,0:T(8,128)(2,1)}, bf16[512,384]{1,0:T(8,128)(2,1)S(1)}, u32[]{:S(2)}, u32[]{:S(2)}) collective-permute-start(bf16[512,384]{1,0:T(8,128)(2,1)} %get-tuple-element.22), channel_id=1, source_target_pairs={{16,0},{24,8},{32,16},{40,24},{48,32},{56,40},{64,48},{72,56},{80,... | collective-permute-start | bytes 1179656 | tf_op jit(solution)/shard_map/ppermute | solution.py:28
  47.7 47.7 %collective-permute-start.5 = (bf16[512,384]{1,0:T(8,128)(2,1)}, bf16[512,384]{1,0:T(8,128)(2,1)S(1)}, u32[]{:S(2)}, u32[]{:S(2)}) collective-permute-start(bf16[512,384]{1,0:T(8,128)(2,1)} %get-tuple-element.23), channel_id=1, source_target_pairs={{0,16},{8,24},{16,32},{24,40},{32,48},{40,56},{48,64},{56,72},{64,... | collective-permute-start | bytes 1179656 | tf_op jit(solution)/shard_map/ppermute | solution.py:28
  52.5 42.9 %collective-permute-start.6 = (bf16[512,384]{1,0:T(8,128)(2,1)}, bf16[512,384]{1,0:T(8,128)(2,1)S(1)}, u32[]{:S(2)}, u32[]{:S(2)}) collective-permute-start(bf16[512,384]{1,0:T(8,128)(2,1)} %get-tuple-element.24), channel_id=1, source_target_pairs={{8,16},{16,8},{24,32},{32,24},{40,48},{48,40},{56,64},{64,56},{72,... | collective-permute-start | bytes 1179656 | tf_op jit(solution)/shard_map/ppermute | solution.py:28
  57.6 37.8 %collective-permute-start.7 = (bf16[512,384]{1,0:T(8,128)(2,1)}, bf16[512,384]{1,0:T(8,128)(2,1)S(1)}, u32[]{:S(2)}, u32[]{:S(2)}) collective-permute-start(bf16[512,384]{1,0:T(8,128)(2,1)} %get-tuple-element.25), channel_id=1, source_target_pairs={{0,8},{8,0},{16,24},{24,16},{32,40},{40,32},{48,56},{56,48},{64,72... | collective-permute-start | bytes 1179656 | tf_op jit(solution)/shard_map/ppermute | solution.py:28
  59.5 4.5 %collective-permute-start.8 = (f32[1,384]{1,0:T(1,128)}, f32[1,384]{1,0:T(1,128)S(1)}, u32[]{:S(2)}, u32[]{:S(2)}) collective-permute-start(f32[1,384]{1,0:T(1,128)} %get-tuple-element.26), channel_id=1, source_target_pairs={{0,256},{256,0},{1,257},{257,1},{2,258},{258,2},{3,259},{259,3},{4... | collective-permute-start | bytes 4616 | tf_op jit(solution)/shard_map/ppermute | solution.py:234

commit v2 on v1

v2 whole, which is shorter than its diff:
```python
import jax
import jax.numpy as jnp
from jax import lax
from jax.experimental import pallas as pl
from jax.experimental.pallas import tpu as pltpu
from jax.sharding import PartitionSpec as P


D = 3072
HD = 96
TB = 128
EB = 128
FR = 256
W = 384
TENSOR = 8
SEQ = 32
SCALE = HD ** (-0.5)
epsilon = 1e-06

PIECES = 5
NT = (((1,), (1,)), ((), ()))
PAIRS = ((0, (0, 96)), (128, (64, 160)))


def permute(array, axis, target):
    size = lax.axis_size(axis)
    pairs = [(i, target(i)) for i in range(size) if 0 <= target(i) < size]
    return lax.ppermute(array, axis, pairs)


def offsets(here):
    core = lax.rem(here, 2)
    toward = 1 - 2 * core
    return (0, toward, -2, 2, -toward)


def blocked(rows, pair):
    first, starts = PAIRS[pair]
    part = rows[:, first : first + 256]
    lane = lax.broadcasted_iota(jnp.int32, part.shape, 1)
    zero = jnp.zeros_like(part)
    return jnp.concatenate(
        [jnp.where((lane >= at) & (lane < at + HD), part, zero) for at in starts], axis=0
    )


def side_by_side(pairs):
    lane = lax.broadcasted_iota(jnp.int32, (TB, 256), 1)
    low = jnp.where(lane < HD, pairs[0][:TB], pairs[0][TB:])
    high = jnp.where(lane < 160, pairs[1][:TB], pairs[1][TB:])
    middle = jnp.where(lane[:, :128] < 64, low[:, 128:], high[:, :128])
    return jnp.concatenate([low[:, :128], middle, high[:, 128:]], axis=1)


def to_rows(columns):
    lane = lax.broadcasted_iota(jnp.int32, (TB, TB), 1)
    tile = jnp.zeros((TB, TB), jnp.float32)
    for index, column in enumerate(columns):
        tile = jnp.where(lane == index, column, tile)
    return tile.T


def split(rows):
    terms = []
    for _ in range(3):
        term = rows.astype(jnp.bfloat16)
        rows = rows - term.astype(jnp.float32)
        terms.append(term)
    return jnp.concatenate(terms, axis=1)


def merge(terms):
    terms = terms.astype(jnp.float32)
    return (terms[:, 0:TB] + terms[:, TB : 2 * TB]) + terms[:, 2 * TB : W]


def pack_kernel(
    k_ref, v_ref, q_ref, go_ref, gain_ref, own_ref, query_ref, grad_ref, row_ref, line, sems
):
    moves = (
        (k_ref, own_ref.at[0:FR]),
        (v_ref, own_ref.at[FR : 2 * FR]),
        (q_ref, query_ref),
        (go_ref, grad_ref),
        (gain_ref, line),
    )
    copies = [
        pltpu.make_async_copy(source, target, sems.at[index])
        for index, (source, target) in enumerate(moves)
    ]
    for copy in copies:
        copy.start()
    for copy in copies:
        copy.wait()
    row_ref[...] = line[...].reshape(1, W)


def forward_kernel(
    start_ref, end_ref, q_ref, go_ref, gain_ref, *rest
):
    pieces = rest[:PIECES]
    attn_ref, probs_ref, stats_ref, norms_ref, scores = rest[PIECES:]
    here = lax.axis_index("seq")
    first = start_ref[0, 0]
    last = end_ref[0, 0]
    rows = q_ref[...]
    results = []
    tops = []
    scales = []
    for pair in range(2):
        at = PAIRS[pair][0]
        block = blocked(rows, pair)
        top = None
        for index, offset in enumerate(offsets(here)):
            frames = 2 * (here + offset)
            product = (
                lax.dot_general(
                    block,
                    pieces[index][0:FR, at : at + 256],
                    NT,
                    preferred_element_type=jnp.float32,
                )
                * SCALE
            )
            for half in range(2):
                allowed = (frames + half >= first) & (frames + half < last)
                bias = jnp.where(allowed, 0.0, -jnp.inf)
                part = product[:, half * EB : (half + 1) * EB] + bias
                scores[pair, :, index * FR + half * EB : index * FR + (half + 1) * EB] = part
                top = part if top is None else jnp.maximum(top, part)
        top = jnp.max(top, axis=1, keepdims=True)
        weights = jnp.exp(scores[pair] - top)
        total = jnp.sum(weights, axis=1, keepdims=True)
        inverse = 1.0 / total
        tops += [top[:TB], top[TB:]]
        scales += [inverse[:TB], inverse[TB:]]
        probs = weights * inverse
        probs_ref[pair] = probs
        probs = probs.astype(jnp.bfloat16)
        acc = None
        for index in range(PIECES):
            part = jnp.dot(
                probs[:, index * FR : (index + 1) * FR],
                pieces[index][FR : 2 * FR, at : at + 256],
                preferred_element_type=jnp.float32,
            )
            acc = part if acc is None else acc + part
        results.append(acc)
    attn = side_by_side(results)
    attn_ref[...] = attn
    scaled = go_ref[...].astype(jnp.float32) * gain_ref[...]
    square = jnp.sum(attn * attn, axis=1, keepdims=True)
    cross = jnp.sum(scaled * attn, axis=1, keepdims=True)
    stats = to_rows([*tops, *scales, square, cross])
    norms_ref[...] = stats[0:8]
    for index in range(TENSOR):
        stats_ref[index] = stats[8:10]


def token_kernel(
    start_ref, end_ref, q_ref, go_ref, gain_ref, attn_ref, probs_ref, norms_ref, stats_ref, *rest
):
    pieces = rest[:PIECES]
    attended_ref, gain_part_ref, gq_ref, sent_ref, grads = rest[PIECES:]
    stats = stats_ref[0]
    for index in range(1, TENSOR):
        stats = stats + stats_ref[index]
    row = lax.broadcasted_iota(jnp.int32, (TB, TB), 0)
    tile = jnp.where(row == 0, stats[0:1], jnp.where(row == 1, stats[1:2], 0.0)).T
    inv = lax.rsqrt(tile[:, 0:1] / D + epsilon)
    mean_cross = inv * tile[:, 1:2] / D
    grad = go_ref[...].astype(jnp.float32)
    gain = gain_ref[...]
    normed = attn_ref[...] * inv
    attended_ref[...] = (normed * gain).astype(jnp.bfloat16)
    gain_part_ref[...] = jnp.broadcast_to(
        jnp.sum(grad * normed, axis=0, keepdims=True)[None], (SEQ, 1, W)
    )
    grad_attn = (inv * (grad * gain - normed * mean_cross)).astype(jnp.bfloat16)
    rows = q_ref[...]
    sent_ref[0:TB] = grad_attn
    sent_ref[TB : 2 * TB] = rows
    grad_q = []
    inners = []
    for pair in range(2):
        at = PAIRS[pair][0]
        cot = blocked(grad_attn, pair)
        inner = None
        for index in range(PIECES):
            span = slice(index * FR, (index + 1) * FR)
            part = lax.dot_general(
                cot,
                pieces[index][FR : 2 * FR, at : at + 256],
                NT,
                preferred_element_type=jnp.float32,
            )
            grads[:, span] = part
            part = probs_ref[pair, :, span] * part
            inner = part if inner is None else inner + part
        inner = jnp.sum(inner, axis=1, keepdims=True)
        inners += [inner[:TB], inner[TB:]]
        acc = None
        for index in range(PIECES):
            span = slice(index * FR, (index + 1) * FR)
            ds = (probs_ref[pair, :, span] * (grads[:, span] - inner)).astype(jnp.bfloat16)
            part = jnp.dot(
                ds, pieces[index][0:FR, at : at + 256], preferred_element_type=jnp.float32
            )
            acc = part if acc is None else acc + part
        grad_q.append(acc)
    gq_ref[...] = (side_by_side(grad_q) * SCALE).astype(jnp.bfloat16)
    band = lax.broadcasted_iota(jnp.int32, (4, TB), 0)
    band = jnp.where(band == 0, start_ref[0, 0], end_ref[0, 0]).astype(jnp.float32)
    sent_ref[2 * TB : 2 * TB + 16] = split(
        jnp.concatenate([norms_ref[...], to_rows(inners)[0:4], band], axis=0)
    )


def frame_kernel(own_ref, *rest):
    tokens = rest[:PIECES]
    gk_ref, gv_ref = rest[PIECES:]
    here = lax.axis_index("seq")
    totals = []
    extras = [merge(tokens[index][2 * TB : 2 * TB + 16]) for index in range(PIECES)]
    for pair in range(2):
        at = PAIRS[pair][0]
        keys = own_ref[0:FR, at : at + 256]
        values = own_ref[FR : 2 * FR, at : at + 256]
        grad_k = None
        for index in range(PIECES):
            extra = extras[index]

            def both(base):
                low = base + 2 * pair
                return jnp.concatenate([extra[low : low + 1], extra[low + 1 : low + 2]], axis=1)

            top, inverse, inner = both(0), both(4), both(8)
            first = jnp.concatenate([extra[12:13]] * 2, axis=1)
            last = jnp.concatenate([extra[13:14]] * 2, axis=1)
            block = blocked(tokens[index][TB : 2 * TB], pair)
            cot = blocked(tokens[index][0:TB], pair)
            scores = (
                lax.dot_general(keys, block, NT, preferred_element_type=jnp.float32) * SCALE
            )
            weights = []
            for half in range(2):
                frame = (2 * here + half).astype(jnp.float32)
                allowed = (frame >= first) & (frame < last)
                weights.append(
                    jnp.exp(scores[half * EB : (half + 1) * EB] - jnp.where(allowed, top, jnp.inf))
                )
            probs = jnp.concatenate(weights, axis=0) * inverse
            grads = lax.dot_general(values, cot, NT, preferred_element_type=jnp.float32)
            ds = (probs * (grads - inner)).astype(jnp.bfloat16)
            part_v = jnp.dot(
                probs.astype(jnp.bfloat16), cot, preferred_element_type=jnp.float32
            )
            part_k = jnp.dot(ds, block, preferred_element_type=jnp.float32)
            if grad_k is None:
                grad_k, grad_v = part_k, part_v
            else:
                grad_k, grad_v = grad_k + part_k, grad_v + part_v
        totals.append((grad_k * SCALE, grad_v))
    for which, out in ((0, gk_ref), (1, gv_ref)):
        low, high = totals[0][which], totals[1][which]
        out[:, 0:128] = low[:, :128].astype(out.dtype)
        out[:, 128:256] = (low[:, 128:] + high[:, :128]).astype(out.dtype)
        out[:, 256:384] = high[:, 128:].astype(out.dtype)


VMEM = pl.BlockSpec(memory_space=pltpu.VMEM)
SMEM = pl.BlockSpec(memory_space=pltpu.SMEM)


def call(kernel, outputs, products, scratch=(), scalars=0, vectors=0):
    return pl.pallas_call(
        kernel,
        out_shape=tuple(jax.ShapeDtypeStruct(shape, dtype) for shape, dtype in outputs),
        in_specs=[SMEM] * scalars + [VMEM] * vectors,
        out_specs=(VMEM,) * len(outputs),
        scratch_shapes=[pltpu.VMEM(shape, jnp.float32) for shape in scratch],
        compiler_params=pltpu.CompilerParams(vmem_limit_bytes=24 << 20),
        cost_estimate=pl.CostEstimate(
            flops=products * 2 * 512 * 1280 * 256,
            bytes_accessed=4 << 20,
            transcendentals=512 * 1280,
        ),
    )


def per_device(queries, keys, values, grad_out, gain, band_start, band_end):
    f32, bf16 = jnp.float32, jnp.bfloat16
    here = lax.axis_index("seq")
    core = lax.rem(here, 2)
    own, query, grad, gain_row = pl.pallas_call(
        pack_kernel,
        out_shape=(
            jax.ShapeDtypeStruct((2 * FR, W), bf16),
            jax.ShapeDtypeStruct((TB, W), bf16),
            jax.ShapeDtypeStruct((TB, W), bf16),
            jax.ShapeDtypeStruct((1, W), f32),
        ),
        in_specs=[pl.BlockSpec(memory_space=pltpu.HBM)] * 5,
        out_specs=(VMEM,) * 4,
        scratch_shapes=[pltpu.VMEM((W,), f32), pltpu.SemaphoreType.DMA((5,))],
        compiler_params=pltpu.CompilerParams(vmem_limit_bytes=24 << 20),
        name="pack",
    )(*[
        pltpu.with_memory_space_constraint(array, pltpu.HBM)
        for array in (keys[0], values[0], queries[0], grad_out[0], gain)
    ])
    below = permute(own, "seq", lambda i: i + 2)
    above = permute(own, "seq", lambda i: i - 2)
    partner = permute(own, "seq", lambda i: i ^ 1)
    beyond = permute(jnp.where(core == 0, above, below), "seq", lambda i: i ^ 1)
    pieces = (own, partner, below, above, beyond)
    whole = (2 * TB, PIECES * FR)
    attn, probs, stats, norms = call(
        forward_kernel,
        (((TB, W), f32), ((2, *whole), f32), ((TENSOR, 2, TB), f32), ((8, TB), f32)),
        2,
        scratch=((2, *whole),),
        scalars=2,
        vectors=3 + PIECES,
    )(band_start, band_end, query, grad, gain_row, *pieces)
    stats = lax.all_to_all(stats, "tensor", 0, 0, tiled=False)
    attended, gain_part, grad_queries, sent = call(
        token_kernel,
        (((TB, W), bf16), ((SEQ, 1, W), f32), ((TB, W), bf16), ((2 * TB + 16, W), bf16)),
        2,
        scratch=(whole,),
        scalars=2,
        vectors=7 + PIECES,
    )(band_start, band_end, query, grad, gain_row, attn, probs, norms, stats, *pieces)
    tokens = (
        sent,
        permute(sent, "seq", lambda i: i ^ 1),
        permute(sent, "seq", lambda i: i + 2),
        permute(sent, "seq", lambda i: i - 2),
        permute(sent, "seq", lambda i: i - 1 if i % 2 == 0 else i + 1),
    )
    gain_sum = jnp.sum(lax.all_to_all(gain_part, "seq", 0, 0, tiled=False), axis=(0, 1))
    gain_other = lax.ppermute(gain_sum, "dp", [(0, 1), (1, 0)])
    grad_keys, grad_values = call(
        frame_kernel, (((FR, W), bf16), ((FR, W), bf16)), 4, vectors=1 + PIECES
    )(own, *tokens)
    grad_gain = gain_sum + gain_other
    return (
        attended[None],
        grad_queries[None],
        grad_keys[None],
        grad_values[None],
        grad_gain,
    )


def solution(mesh):
    return jax.shard_map(
        per_device,
        mesh=mesh,
        in_specs=(
            P("dp", "seq", "tensor"),
            P("dp", "seq", "tensor"),
            P("dp", "seq", "tensor"),
            P("dp", "seq", "tensor"),
            P("tensor"),
            P("dp", "seq"),
            P("dp", "seq"),
        ),
        out_specs=(
            P("dp", "seq", "tensor"),
            P("dp", "seq", "tensor"),
            P("dp", "seq", "tensor"),
            P("dp", "seq", "tensor"),
            P("tensor"),
        ),
        check_vma=False,
    )
```

time: 98.1 us -> 89.8 us (0.915)
  the two profiles are of different devices: /device:TPU:1 before, /device:TPU:2 now
where the time goes in v2:
time: 89.8 us; the launch traced here: 89.4 us
  blocking collectives  44.4 us (49%)
  starting transfers between devices  24.9 us (28%)
  waiting for transfers between devices  8.82 us (10%)
  Pallas kernels  8.53 us (9%)
  between operations  2.04 us (2%)
    all_to_all x1, blocking collectives, per_device(): lax.all_to_all(gain_part, 'seq', 0, 0, tiled=False)  30.9 us
    ppermute x8, starting transfers between devices, permute(): return lax.ppermute(array, axis, pairs)  21.6 us
    all_to_all x1, blocking collectives, per_device(): stats = lax.all_to_all(stats, 'tensor', 0, 0, tiled=False)  13.5 us
    ppermute x8, waiting for transfers between devices, permute(): return lax.ppermute(array, axis, pairs)  6.7 us
    ppermute x1, starting transfers between devices, per_device(): gain_other = lax.ppermute(gain_sum, 'dp', [(0, 1), (1, 0)])  3.34 us
    pallas_call x1, Pallas kernels, per_device(): call(frame_kernel, (((FR, W), bf16), ((FR, W), bf16)), 4, vectors=1 + PIE...  3 us
    pallas_call x1, Pallas kernels, per_device(): call(token_kernel, (((TB, W), bf16), ((SEQ, 1, W), f32), ((TB, W), bf16),...  2.45 us
    ppermute x1, waiting for transfers between devices, per_device(): gain_other = lax.ppermute(gain_sum, 'dp', [(0, 1), (1, 0)])  2.13 us
  transfers between devices with their start and end apart: 9, of which 4 were waited for; matrix products, arithmetic and copies ran while one was open for 1% of the time, Pallas kernels for 0%

profile of v2, /device:TPU:2, one launch (start us, length us, event | category | flops | bytes accessed | tf_op | source)
XLA Modules:
  0.0 89.4 jit_solution(335721700330318651)
XLA Ops:
  0.6 1.2 %pack.1 = (bf16[512,384]{1,0:T(8,128)(2,1)S(1)}, bf16[128,384]{1,0:T(8,128)(2,1)S(1)}, bf16[128,384]{1,0:T(8,128)(2,1)S(1)}, f32[1,384]{1,0:T(1,128)S(1)}) custom-call(bf16[256,384]{1,0:T(8,128)(2,1)} %bitcast.8, bf16[256,384]{1,0:T(8,128)(2,1)} %bitcast.9, bf16[128,384]{1,0:T(8,128)(2,1)} %bitcast.10, bf16[128,384]{1,0:T(8,128)(2,1)} %bitcast.11, f32[384]{0:T(512)} %gain_ref.1), custom_call_target="tpu_custom_call" | custom-call | tf_op jit(solution)/shard_map/pack/pallas_call | solution.py:295
  1.8 1.3 %collective-permute-start.2 = (bf16[512,384]{1,0:T(8,128)(2,1)S(1)}, bf16[512,384]{1,0:T(8,128)(2,1)S(1)}, u32[]{:S(2)}, u32[]{:S(2)}) collective-permute-start(bf16[512,384]{1,0:T(8,128)(2,1)S(1)} %get-tuple-element.22.rest_0_.own_ref), channel_id=1, source_target_pairs={{16,0},{24,8},{32,16},{40,24},{48,32},{56,40},{64,48},{72,56},{80,... | collective-permute-start | bytes 1179656 | tf_op jit(solution)/shard_map/ppermute | solution.py:28
  3.1 4.6 %collective-permute-start.1 = (bf16[512,384]{1,0:T(8,128)(2,1)S(1)}, bf16[512,384]{1,0:T(8,128)(2,1)S(1)}, u32[]{:S(2)}, u32[]{:S(2)}) collective-permute-start(bf16[512,384]{1,0:T(8,128)(2,1)S(1)} %get-tuple-element.22.rest_0_.own_ref), channel_id=1, source_target_pairs={{0,16},{8,24},{16,32},{24,40},{32,48},{40,56},{48,64},{56,72},{64,... | collective-permute-start | bytes 1179656 | tf_op jit(solution)/shard_map/ppermute | solution.py:28
  7.7 1.9 %collective-permute-start = (bf16[512,384]{1,0:T(8,128)(2,1)S(1)}, bf16[512,384]{1,0:T(8,128)(2,1)S(1)}, u32[]{:S(2)}, u32[]{:S(2)}) collective-permute-start(bf16[512,384]{1,0:T(8,128)(2,1)S(1)} %get-tuple-element.22.rest_0_.own_ref), channel_id=1, source_target_pairs={{0,8},{8,0},{16,24},{24,16},{32,40},{40,32},{48,56},{56,48},{64,72... | collective-permute-start | bytes 1179656 | tf_op jit(solution)/shard_map/ppermute | solution.py:28
  9.6 5.1 %collective-permute-done.2.rest_3_ = bf16[512,384]{1,0:T(8,128)(2,1)S(1)} collective-permute-done((bf16[512,384]{1,0:T(8,128)(2,1)S(1)}, bf16[512,384]{1,0:T(8,128)(2,1)S(1)}, u32[]{:S(2)}, u32[]{:S(2)}) %collective-permute-start.2) | collective-permute-done | bytes 393248 | tf_op jit(solution)/shard_map/ppermute | solution.py:28
  14.8 1.2 %collective-permute-done.1.rest_2_ = bf16[512,384]{1,0:T(8,128)(2,1)S(1)} collective-permute-done((bf16[512,384]{1,0:T(8,128)(2,1)S(1)}, bf16[512,384]{1,0:T(8,128)(2,1)S(1)}, u32[]{:S(2)}, u32[]{:S(2)}) %collective-permute-start.1) | collective-permute-done | bytes 393248 | tf_op jit(solution)/shard_map/ppermute | solution.py:28
  16.0 1.9 %collective-permute-start.3 = (bf16[512,384]{1,0:T(8,128)(2,1)S(1)}, bf16[512,384]{1,0:T(8,128)(2,1)S(1)}, u32[]{:S(2)}, u32[]{:S(2)}) collective-permute-start(bf16[512,384]{1,0:T(8,128)(2,1)S(1)} %broadcast_select_fusion), channel_id=1, source_target_pairs={{0,8},{8,0},{16,24},{24,16},{32,40},{40,32},{48,56},{56,48},{64,72... | collective-permute-start | bytes 1179656 | tf_op jit(solution)/shard_map/ppermute | solution.py:28
  19.2 0.0 collective-permute-done.rest_1_
  19.2 0.4 collective-permute-done.3.rest_4_
  19.6 1.9 %shard_map.110 = (f32[128,384]{1,0:T(8,128)S(1)}, f32[2,256,1280]{2,1,0:T(8,128)S(1)}, f32[8,2,128]{2,1,0:T(2,128)S(1)}, f32[8,128]{1,0:T(8,128)S(1)}) custom-call(s32[1,1]{1,0:T(1,128)S(6)} %copy.12.start_ref, s32[1,1]{1,0:T(1,128)S(6)} %copy.13.end_ref, bf16[128,384]{1,0:T(8,128)(2,1)S(1)} %get-tuple-element.19.q_ref, ...), custom_call_target="tpu_custom_call" | custom-call | flops 671088640 | bytes 4194304 | tf_op jit(solution)/shard_map/pallas_call | solution.py:318
  21.5 13.5 %all_to_all.10.stats_ref = f32[8,2,128]{2,1,0:T(2,128)S(1)} all-to-all(f32[8,2,128]{2,1,0:T(2,128)S(1)} %get-tuple-element.26), channel_id=1, replica_groups=mesh['dp'=2,'seq'=32,'tensor'=8] {'tensor'}, dimensions={0} | all-to-all | bytes 16384 | tf_op jit(solution)/shard_map/all_to_all | solution.py:326
  35.0 2.4 %shard_map.111 = (bf16[128,384]{1,0:T(8,128)(2,1)}, f32[32,1,384]{2,1,0:T(1,128)S(1)}, bf16[128,384]{1,0:T(8,128)(2,1)}, bf16[272,384]{1,0:T(8,128)(2,1)S(1)}) custom-call(s32[1,1]{1,0:T(1,128)S(6)} %copy.12.start_ref, s32[1,1]{1,0:T(1,128)S(6)} %copy.13.end_ref, bf16[128,384]{1,0:T(8,128)(2,1)S(1)} %get-tuple-element.19.q_ref, ...), custom_call_target="tpu_custom_call" | custom-call | flops 671088640 | bytes 4194304 | tf_op jit(solution)/shard_map/pallas_call | solution.py:327
  37.5 0.7 collective-permute-start.7
  38.1 1.3 %collective-permute-start.6 = (bf16[272,384]{1,0:T(8,128)(2,1)S(1)}, bf16[272,384]{1,0:T(8,128)(2,1)S(1)}, u32[]{:S(2)}, u32[]{:S(2)}) collective-permute-start(bf16[272,384]{1,0:T(8,128)(2,1)S(1)} %get-tuple-element.29.rest_0_), channel_id=1, source_target_pairs={{16,0},{24,8},{32,16},{40,24},{48,32},{56,40},{64,48},{72,56},{80,... | collective-permute-start | bytes 626696 | tf_op jit(solution)/shard_map/ppermute | solution.py:28
  39.4 6.3 %collective-permute-start.5 = (bf16[272,384]{1,0:T(8,128)(2,1)S(1)}, bf16[272,384]{1,0:T(8,128)(2,1)S(1)}, u32[]{:S(2)}, u32[]{:S(2)}) collective-permute-start(bf16[272,384]{1,0:T(8,128)(2,1)S(1)} %get-tuple-element.29.rest_0_), channel_id=1, source_target_pairs={{0,16},{8,24},{16,32},{24,40},{32,48},{40,56},{48,64},{56,72},{64,... | collective-permute-start | bytes 626696 | tf_op jit(solution)/shard_map/ppermute | solution.py:28
  45.7 3.6 %collective-permute-start.4 = (bf16[272,384]{1,0:T(8,128)(2,1)S(1)}, bf16[272,384]{1,0:T(8,128)(2,1)S(1)}, u32[]{:S(2)}, u32[]{:S(2)}) collective-permute-start(bf16[272,384]{1,0:T(8,128)(2,1)S(1)} %get-tuple-element.29.rest_0_), channel_id=1, source_target_pairs={{0,8},{8,0},{16,24},{24,16},{32,40},{40,32},{48,56},{56,48},{64,72... | collective-permute-start | bytes 626696 | tf_op jit(solution)/shard_map/ppermute | solution.py:28
  49.4 30.9 %all_to_all.11 = f32[32,1,384]{2,1,0:T(1,128)S(1)} all-to-all(f32[32,1,384]{2,1,0:T(1,128)S(1)} %get-tuple-element.32), channel_id=1, replica_groups=mesh['dp'=2,'seq'=32,'tensor'=8] {'seq'}, dimensions={0} | all-to-all | bytes 98304 | tf_op jit(solution)/shard_map/all_to_all | solution.py:342
  80.3 0.1 reduce_sum.9
  80.3 3.3 %collective-permute-start.8 = (f32[384]{0:T(512)S(1)}, f32[384]{0:T(512)S(1)}, u32[]{:S(2)}, u32[]{:S(2)}) collective-permute-start(f32[384]{0:T(512)S(1)} %reduce_sum.9), channel_id=1, source_target_pairs={{0,256},{256,0},{1,257},{257,1},{2,258},{258,2},{3,259},{259,3},{4... | collective-permute-start | bytes 4616 | tf_op jit(solution)/shard_map/ppermute | solution.py:343
  83.7 2.1 %collective-permute-done.8 = f32[384]{0:T(512)S(1)} collective-permute-done((f32[384]{0:T(512)S(1)}, f32[384]{0:T(512)S(1)}, u32[]{:S(2)}, u32[]{:S(2)}) %collective-permute-start.8) | collective-permute-done | bytes 1568 | tf_op jit(solution)/shard_map/ppermute | solution.py:343
  85.8 0.6 add.3
  86.4 0.0 collective-permute-done.7.rest_4_
  86.4 0.0 collective-permute-done.6.rest_3_
  86.4 0.0 collective-permute-done.5.rest_2_
  86.4 0.0 collective-permute-done.4.rest_1_
  86.4 3.0 %shard_map.112 = (bf16[256,384]{1,0:T(8,128)(2,1)}, bf16[256,384]{1,0:T(8,128)(2,1)}) custom-call(bf16[512,384]{1,0:T(8,128)(2,1)S(1)} %get-tuple-element.22.rest_0_.own_ref, bf16[272,384]{1,0:T(8,128)(2,1)S(1)} %get-tuple-element.29.rest_0_, bf16[272,384]{1,0:T(8,128)(2,1)S(1)} %collective-permute-done.4.rest_1_, ...), custom_call_target="tpu_custom_call" | custom-call | flops 1342177280 | bytes 4194304 | tf_op jit(solution)/shard_map/pallas_call | solution.py:344
  (1 shorter events, 0.0 us)
Async XLA Ops:
  1.8 12.9 %collective-permute-start.2 = (bf16[512,384]{1,0:T(8,128)(2,1)S(1)}, bf16[512,384]{1,0:T(8,128)(2,1)S(1)}, u32[]{:S(2)}, u32[]{:S(2)}) collective-permute-start(bf16[512,384]{1,0:T(8,128)(2,1)S(1)} %get-tuple-element.22.rest_0_.own_ref), channel_id=1, source_target_pairs={{16,0},{24,8},{32,16},{40,24},{48,32},{56,40},{64,48},{72,56},{80,... | collective-permute-start | bytes 1179656 | tf_op jit(solution)/shard_map/ppermute | solution.py:28
  3.1 12.8 %collective-permute-start.1 = (bf16[512,384]{1,0:T(8,128)(2,1)S(1)}, bf16[512,384]{1,0:T(8,128)(2,1)S(1)}, u32[]{:S(2)}, u32[]{:S(2)}) collective-permute-start(bf16[512,384]{1,0:T(8,128)(2,1)S(1)} %get-tuple-element.22.rest_0_.own_ref), channel_id=1, source_target_pairs={{0,16},{8,24},{16,32},{24,40},{32,48},{40,56},{48,64},{56,72},{64,... | collective-permute-start | bytes 1179656 | tf_op jit(solution)/shard_map/ppermute | solution.py:28
  7.7 11.5 %collective-permute-start = (bf16[512,384]{1,0:T(8,128)(2,1)S(1)}, bf16[512,384]{1,0:T(8,128)(2,1)S(1)}, u32[]{:S(2)}, u32[]{:S(2)}) collective-permute-start(bf16[512,384]{1,0:T(8,128)(2,1)S(1)} %get-tuple-element.22.rest_0_.own_ref), channel_id=1, source_target_pairs={{0,8},{8,0},{16,24},{24,16},{32,40},{40,32},{48,56},{56,48},{64,72... | collective-permute-start | bytes 1179656 | tf_op jit(solution)/shard_map/ppermute | solution.py:28
  16.0 3.6 %collective-permute-start.3 = (bf16[512,384]{1,0:T(8,128)(2,1)S(1)}, bf16[512,384]{1,0:T(8,128)(2,1)S(1)}, u32[]{:S(2)}, u32[]{:S(2)}) collective-permute-start(bf16[512,384]{1,0:T(8,128)(2,1)S(1)} %broadcast_select_fusion), channel_id=1, source_target_pairs={{0,8},{8,0},{16,24},{24,16},{32,40},{40,32},{48,56},{56,48},{64,72... | collective-permute-start | bytes 1179656 | tf_op jit(solution)/shard_map/ppermute | solution.py:28
  37.5 48.9 %collective-permute-start.7 = (bf16[272,384]{1,0:T(8,128)(2,1)S(1)}, bf16[272,384]{1,0:T(8,128)(2,1)S(1)}, u32[]{:S(2)}, u32[]{:S(2)}) collective-permute-start(bf16[272,384]{1,0:T(8,128)(2,1)S(1)} %get-tuple-element.29.rest_0_), channel_id=1, source_target_pairs={{8,16},{16,8},{24,32},{32,24},{40,48},{48,40},{56,64},{64,56},{72,... | collective-permute-start | bytes 626696 | tf_op jit(solution)/shard_map/ppermute | solution.py:28
  38.1 48.2 %collective-permute-start.6 = (bf16[272,384]{1,0:T(8,128)(2,1)S(1)}, bf16[272,384]{1,0:T(8,128)(2,1)S(1)}, u32[]{:S(2)}, u32[]{:S(2)}) collective-permute-start(bf16[272,384]{1,0:T(8,128)(2,1)S(1)} %get-tuple-element.29.rest_0_), channel_id=1, source_target_pairs={{16,0},{24,8},{32,16},{40,24},{48,32},{56,40},{64,48},{72,56},{80,... | collective-permute-start | bytes 626696 | tf_op jit(solution)/shard_map/ppermute | solution.py:28
  39.4 46.9 %collective-permute-start.5 = (bf16[272,384]{1,0:T(8,128)(2,1)S(1)}, bf16[272,384]{1,0:T(8,128)(2,1)S(1)}, u32[]{:S(2)}, u32[]{:S(2)}) collective-permute-start(bf16[272,384]{1,0:T(8,128)(2,1)S(1)} %get-tuple-element.29.rest_0_), channel_id=1, source_target_pairs={{0,16},{8,24},{16,32},{24,40},{32,48},{40,56},{48,64},{56,72},{64,... | collective-permute-start | bytes 626696 | tf_op jit(solution)/shard_map/ppermute | solution.py:28
  45.7 40.7 %collective-permute-start.4 = (bf16[272,384]{1,0:T(8,128)(2,1)S(1)}, bf16[272,384]{1,0:T(8,128)(2,1)S(1)}, u32[]{:S(2)}, u32[]{:S(2)}) collective-permute-start(bf16[272,384]{1,0:T(8,128)(2,1)S(1)} %get-tuple-element.29.rest_0_), channel_id=1, source_target_pairs={{0,8},{8,0},{16,24},{24,16},{32,40},{40,32},{48,56},{56,48},{64,72... | collective-permute-start | bytes 626696 | tf_op jit(solution)/shard_map/ppermute | solution.py:28
  80.3 5.5 %collective-permute-start.8 = (f32[384]{0:T(512)S(1)}, f32[384]{0:T(512)S(1)}, u32[]{:S(2)}, u32[]{:S(2)}) collective-permute-start(f32[384]{0:T(512)S(1)} %reduce_sum.9), channel_id=1, source_target_pairs={{0,256},{256,0},{1,257},{257,1},{2,258},{258,2},{3,259},{259,3},{4... | collective-permute-start | bytes 4616 | tf_op jit(solution)/shard_map/ppermute | solution.py:343

commit v3 on v2

--- a/solution.py
+++ b/solution.py
@@ -18,6 +18,7 @@
 epsilon = 1e-06
 
 PIECES = 5
+EARLY = 3
 NT = (((1,), (1,)), ((), ()))
 PAIRS = ((0, (0, 96)), (128, (64, 160)))
 
@@ -216,19 +217,16 @@
     )
 
 
-def frame_kernel(own_ref, *rest):
-    tokens = rest[:PIECES]
-    gk_ref, gv_ref = rest[PIECES:]
+def frame_sums(own_ref, tokens, sums):
     here = lax.axis_index("seq")
     totals = []
-    extras = [merge(tokens[index][2 * TB : 2 * TB + 16]) for index in range(PIECES)]
+    extras = [merge(token[2 * TB : 2 * TB + 16]) for token in tokens]
     for pair in range(2):
         at = PAIRS[pair][0]
         keys = own_ref[0:FR, at : at + 256]
         values = own_ref[FR : 2 * FR, at : at + 256]
-        grad_k = None
-        for index in range(PIECES):
-            extra = extras[index]
+        grad_k, grad_v = sums[pair]
+        for index, extra in enumerate(extras):
 
             def both(base):
                 low = base + 2 * pair
@@ -260,9 +258,24 @@
                 grad_k, grad_v = part_k, part_v
             else:
                 grad_k, grad_v = grad_k + part_k, grad_v + part_v
-        totals.append((grad_k * SCALE, grad_v))
-    for which, out in ((0, gk_ref), (1, gv_ref)):
-        low, high = totals[0][which], totals[1][which]
+        totals.append((grad_k, grad_v))
+    return totals
+
+
+def first_frame_kernel(own_ref, *rest):
+    totals = frame_sums(own_ref, rest[:EARLY], [(None, None)] * 2)
+    for pair in range(2):
+        for which in range(2):
+            rest[EARLY][pair, which] = totals[pair][which]
+
+
+def last_frame_kernel(own_ref, sums_ref, *rest):
+    tokens = rest[: PIECES - EARLY]
+    outs = rest[PIECES - EARLY :]
+    sums = [(sums_ref[pair, 0], sums_ref[pair, 1]) for pair in range(2)]
+    totals = frame_sums(own_ref, tokens, sums)
+    for which, (out, scale) in enumerate(zip(outs, (SCALE, 1.0))):
+        low, high = totals[0][which] * scale, totals[1][which] * scale
         out[:, 0:128] = low[:, :128].astype(out.dtype)
         out[:, 128:256] = (low[:, 128:] + high[:, :128]).astype(out.dtype)
         out[:, 256:384] = high[:, 128:].astype(out.dtype)
@@ -332,6 +345,8 @@
         scalars=2,
         vectors=7 + PIECES,
     )(band_start, band_end, query, grad, gain_row, attn, probs, norms, stats, *pieces)
+    spread = lax.all_to_all(gain_part, "seq", 0, 0, tiled=False)
+    gain_sum = jnp.sum(spread, axis=(0, 1))
     tokens = (
         sent,
         permute(sent, "seq", lambda i: i ^ 1),
@@ -339,11 +354,13 @@
         permute(sent, "seq", lambda i: i - 2),
         permute(sent, "seq", lambda i: i - 1 if i % 2 == 0 else i + 1),
     )
-    gain_sum = jnp.sum(lax.all_to_all(gain_part, "seq", 0, 0, tiled=False), axis=(0, 1))
     gain_other = lax.ppermute(gain_sum, "dp", [(0, 1), (1, 0)])
+    (sums,) = call(
+        first_frame_kernel, (((2, 2, FR, 256), f32),), 4, vectors=1 + EARLY
+    )(own, *tokens[:EARLY])
     grad_keys, grad_values = call(
-        frame_kernel, (((FR, W), bf16), ((FR, W), bf16)), 4, vectors=1 + PIECES
-    )(own, *tokens)
+        last_frame_kernel, (((FR, W), bf16), ((FR, W), bf16)), 4, vectors=2 + PIECES - EARLY
+    )(own, sums, *tokens[EARLY:])
     grad_gain = gain_sum + gain_other
     return (
         attended[None],

time: 89.8 us -> 83.8 us (0.933)
  blocking collectives: 44.4 us -> 13.5 us
  starting transfers between devices: 24.9 us -> 37.8 us
  waiting for transfers between devices: 8.82 us -> 20.5 us
    all_to_all x1 -> x0, blocking collectives: 30.9 us -> none  [per_device(): lax.all_to_all(gain_part, 'seq', 0, 0, tiled=False)]
    all_to_all x0 -> x1, starting transfers between devices: none -> 16.5 us  [per_device(): spread = lax.all_to_all(gain_part, 'seq', 0, 0, tiled=False)]
    all_to_all x0 -> x1, waiting for transfers between devices: none -> 11.7 us  [per_device(): spread = lax.all_to_all(gain_part, 'seq', 0, 0, tiled=False)]
    ppermute x8, starting transfers between devices: 21.6 us -> 18 us  [permute(): return lax.ppermute(array, axis, pairs)]
    pallas_call x1 -> x2, Pallas kernels: 3 us -> 3.2 us  [the longest x1 1.83 us: per_device(): call(last_frame_kernel, (((FR, W), bf16), ((FR, W), bf16)), 4, vectors=2...]
  transfers between devices with their start and end apart: 9 -> 10, of which waited for: 4 -> 5; matrix products, arithmetic and copies ran while one was open for 1% -> 1% of each run, Pallas kernels for 0% -> 2%
where the time goes in v3:
time: 83.8 us; the launch traced here: 83.3 us
  starting transfers between devices  37.8 us (45%)
  waiting for transfers between devices  20.5 us (24%)
  blocking collectives  13.5 us (16%)
  Pallas kernels  8.72 us (10%)
  between operations  2.06 us (2%)
    ppermute x8, starting transfers between devices, permute(): return lax.ppermute(array, axis, pairs)  18 us
    all_to_all x1, starting transfers between devices, per_device(): spread = lax.all_to_all(gain_part, 'seq', 0, 0, tiled=False)  16.5 us
    all_to_all x1, blocking collectives, per_device(): stats = lax.all_to_all(stats, 'tensor', 0, 0, tiled=False)  13.5 us
    all_to_all x1, waiting for transfers between devices, per_device(): spread = lax.all_to_all(gain_part, 'seq', 0, 0, tiled=False)  11.7 us
    ppermute x8, waiting for transfers between devices, permute(): return lax.ppermute(array, axis, pairs)  6.7 us
    ppermute x1, starting transfers between devices, per_device(): gain_other = lax.ppermute(gain_sum, 'dp', [(0, 1), (1, 0)])  3.34 us
    pallas_call x1, Pallas kernels, per_device(): call(token_kernel, (((TB, W), bf16), ((SEQ, 1, W), f32), ((TB, W), bf16),...  2.45 us
    ppermute x1, waiting for transfers between devices, per_device(): gain_other = lax.ppermute(gain_sum, 'dp', [(0, 1), (1, 0)])  2.13 us
  transfers between devices with their start and end apart: 10, of which 5 were waited for; matrix products, arithmetic and copies ran while one was open for 1% of the time, Pallas kernels for 2%

profile of v3, /device:TPU:2, one launch (start us, length us, event | category | flops | bytes accessed | tf_op | source)
XLA Modules:
  0.0 83.3 jit_solution(11836995907084102743)
XLA Ops:
  0.6 1.2 %pack.1 = (bf16[512,384]{1,0:T(8,128)(2,1)S(1)}, bf16[128,384]{1,0:T(8,128)(2,1)S(1)}, bf16[128,384]{1,0:T(8,128)(2,1)S(1)}, f32[1,384]{1,0:T(1,128)S(1)}) custom-call(bf16[256,384]{1,0:T(8,128)(2,1)} %bitcast.8, bf16[256,384]{1,0:T(8,128)(2,1)} %bitcast.9, bf16[128,384]{1,0:T(8,128)(2,1)} %bitcast.10, bf16[128,384]{1,0:T(8,128)(2,1)} %bitcast.11, f32[384]{0:T(512)} %gain_ref.1), custom_call_target="tpu_custom_call" | custom-call | tf_op jit(solution)/shard_map/pack/pallas_call | solution.py:308
  1.8 1.3 %collective-permute-start.2 = (bf16[512,384]{1,0:T(8,128)(2,1)S(1)}, bf16[512,384]{1,0:T(8,128)(2,1)S(1)}, u32[]{:S(2)}, u32[]{:S(2)}) collective-permute-start(bf16[512,384]{1,0:T(8,128)(2,1)S(1)} %get-tuple-element.22.rest_0_.own_ref), channel_id=1, source_target_pairs={{16,0},{24,8},{32,16},{40,24},{48,32},{56,40},{64,48},{72,56},{80,... | collective-permute-start | bytes 1179656 | tf_op jit(solution)/shard_map/ppermute | solution.py:29
  3.1 4.6 %collective-permute-start.1 = (bf16[512,384]{1,0:T(8,128)(2,1)S(1)}, bf16[512,384]{1,0:T(8,128)(2,1)S(1)}, u32[]{:S(2)}, u32[]{:S(2)}) collective-permute-start(bf16[512,384]{1,0:T(8,128)(2,1)S(1)} %get-tuple-element.22.rest_0_.own_ref), channel_id=1, source_target_pairs={{0,16},{8,24},{16,32},{24,40},{32,48},{40,56},{48,64},{56,72},{64,... | collective-permute-start | bytes 1179656 | tf_op jit(solution)/shard_map/ppermute | solution.py:29
  7.7 1.9 %collective-permute-start = (bf16[512,384]{1,0:T(8,128)(2,1)S(1)}, bf16[512,384]{1,0:T(8,128)(2,1)S(1)}, u32[]{:S(2)}, u32[]{:S(2)}) collective-permute-start(bf16[512,384]{1,0:T(8,128)(2,1)S(1)} %get-tuple-element.22.rest_0_.own_ref), channel_id=1, source_target_pairs={{0,8},{8,0},{16,24},{24,16},{32,40},{40,32},{48,56},{56,48},{64,72... | collective-permute-start | bytes 1179656 | tf_op jit(solution)/shard_map/ppermute | solution.py:29
  9.6 5.1 %collective-permute-done.2.rest_3_ = bf16[512,384]{1,0:T(8,128)(2,1)S(1)} collective-permute-done((bf16[512,384]{1,0:T(8,128)(2,1)S(1)}, bf16[512,384]{1,0:T(8,128)(2,1)S(1)}, u32[]{:S(2)}, u32[]{:S(2)}) %collective-permute-start.2) | collective-permute-done | bytes 393248 | tf_op jit(solution)/shard_map/ppermute | solution.py:29
  14.8 1.2 %collective-permute-done.1.rest_2_ = bf16[512,384]{1,0:T(8,128)(2,1)S(1)} collective-permute-done((bf16[512,384]{1,0:T(8,128)(2,1)S(1)}, bf16[512,384]{1,0:T(8,128)(2,1)S(1)}, u32[]{:S(2)}, u32[]{:S(2)}) %collective-permute-start.1) | collective-permute-done | bytes 393248 | tf_op jit(solution)/shard_map/ppermute | solution.py:29
  16.0 1.9 %collective-permute-start.3 = (bf16[512,384]{1,0:T(8,128)(2,1)S(1)}, bf16[512,384]{1,0:T(8,128)(2,1)S(1)}, u32[]{:S(2)}, u32[]{:S(2)}) collective-permute-start(bf16[512,384]{1,0:T(8,128)(2,1)S(1)} %broadcast_select_fusion), channel_id=1, source_target_pairs={{0,8},{8,0},{16,24},{24,16},{32,40},{40,32},{48,56},{56,48},{64,72... | collective-permute-start | bytes 1179656 | tf_op jit(solution)/shard_map/ppermute | solution.py:29
  19.2 0.0 collective-permute-done.rest_1_
  19.2 0.4 collective-permute-done.3.rest_4_
  19.6 1.9 %shard_map.110 = (f32[128,384]{1,0:T(8,128)S(1)}, f32[2,256,1280]{2,1,0:T(8,128)S(1)}, f32[8,2,128]{2,1,0:T(2,128)S(1)}, f32[8,128]{1,0:T(8,128)S(1)}) custom-call(s32[1,1]{1,0:T(1,128)S(6)} %copy.12.start_ref, s32[1,1]{1,0:T(1,128)S(6)} %copy.13.end_ref, bf16[128,384]{1,0:T(8,128)(2,1)S(1)} %get-tuple-element.19.q_ref, ...), custom_call_target="tpu_custom_call" | custom-call | flops 671088640 | bytes 4194304 | tf_op jit(solution)/shard_map/pallas_call | solution.py:331
  21.5 13.5 %all_to_all.10.stats_ref = f32[8,2,128]{2,1,0:T(2,128)S(1)} all-to-all(f32[8,2,128]{2,1,0:T(2,128)S(1)} %get-tuple-element.26), channel_id=1, replica_groups=mesh['dp'=2,'seq'=32,'tensor'=8] {'tensor'}, dimensions={0} | all-to-all | bytes 16384 | tf_op jit(solution)/shard_map/all_to_all | solution.py:339
  35.0 2.4 %shard_map.111 = (bf16[128,384]{1,0:T(8,128)(2,1)}, f32[32,1,384]{2,1,0:T(1,128)}, bf16[128,384]{1,0:T(8,128)(2,1)}, bf16[272,384]{1,0:T(8,128)(2,1)S(1)}) custom-call(s32[1,1]{1,0:T(1,128)S(6)} %copy.12.start_ref, s32[1,1]{1,0:T(1,128)S(6)} %copy.13.end_ref, bf16[128,384]{1,0:T(8,128)(2,1)S(1)} %get-tuple-element.19.q_ref, ...), custom_call_target="tpu_custom_call" | custom-call | flops 671088640 | bytes 4194304 | tf_op jit(solution)/shard_map/pallas_call | solution.py:340
  37.5 4.4 %collective-permute-start.5 = (bf16[272,384]{1,0:T(8,128)(2,1)S(1)}, bf16[272,384]{1,0:T(8,128)(2,1)S(1)}, u32[]{:S(2)}, u32[]{:S(2)}) collective-permute-start(bf16[272,384]{1,0:T(8,128)(2,1)S(1)} %get-tuple-element.29.rest_0_), channel_id=1, source_target_pairs={{0,16},{8,24},{16,32},{24,40},{32,48},{40,56},{48,64},{56,72},{64,... | collective-permute-start | bytes 626696 | tf_op jit(solution)/shard_map/ppermute | solution.py:29
  41.9 1.9 %collective-permute-start.4 = (bf16[272,384]{1,0:T(8,128)(2,1)S(1)}, bf16[272,384]{1,0:T(8,128)(2,1)S(1)}, u32[]{:S(2)}, u32[]{:S(2)}) collective-permute-start(bf16[272,384]{1,0:T(8,128)(2,1)S(1)} %get-tuple-element.29.rest_0_), channel_id=1, source_target_pairs={{0,8},{8,0},{16,24},{24,16},{32,40},{40,32},{48,56},{56,48},{64,72... | collective-permute-start | bytes 626696 | tf_op jit(solution)/shard_map/ppermute | solution.py:29
  43.8 16.5 %all-to-all-start.1 = ((f32[32,1,384]{2,1,0:T(1,128)}), f32[32,1,384]{2,1,0:T(1,128)S(1)}, u32[]{:S(2)}, u32[]{:S(2)}) async-start(f32[32,1,384]{2,1,0:T(1,128)} %get-tuple-element.32), calls=%async_computation.1 | async-start | bytes 98304 | tf_op jit(solution)/shard_map/all_to_all | solution.py:348
  60.3 0.7 collective-permute-start.7
  61.0 1.3 %collective-permute-start.6 = (bf16[272,384]{1,0:T(8,128)(2,1)S(1)}, bf16[272,384]{1,0:T(8,128)(2,1)S(1)}, u32[]{:S(2)}, u32[]{:S(2)}) collective-permute-start(bf16[272,384]{1,0:T(8,128)(2,1)S(1)} %get-tuple-element.29.rest_0_), channel_id=1, source_target_pairs={{16,0},{24,8},{32,16},{40,24},{48,32},{56,40},{64,48},{72,56},{80,... | collective-permute-start | bytes 626696 | tf_op jit(solution)/shard_map/ppermute | solution.py:29
  62.3 11.7 %all-to-all-done.1 = f32[32,1,384]{2,1,0:T(1,128)S(1)} async-done(((f32[32,1,384]{2,1,0:T(1,128)}), f32[32,1,384]{2,1,0:T(1,128)S(1)}, u32[]{:S(2)}, u32[]{:S(2)}) %all-to-all-start.1) | async-done | bytes 49184 | tf_op jit(solution)/shard_map/all_to_all | solution.py:348
  74.0 0.1 reduce_sum.9
  74.0 3.3 %collective-permute-start.8 = (f32[384]{0:T(512)S(1)}, f32[384]{0:T(512)S(1)}, u32[]{:S(2)}, u32[]{:S(2)}) collective-permute-start(f32[384]{0:T(512)S(1)} %reduce_sum.9), channel_id=1, source_target_pairs={{0,256},{256,0},{1,257},{257,1},{2,258},{258,2},{3,259},{259,3},{4... | collective-permute-start | bytes 4616 | tf_op jit(solution)/shard_map/ppermute | solution.py:357
  77.4 2.1 %collective-permute-done.8 = f32[384]{0:T(512)S(1)} collective-permute-done((f32[384]{0:T(512)S(1)}, f32[384]{0:T(512)S(1)}, u32[]{:S(2)}, u32[]{:S(2)}) %collective-permute-start.8) | collective-permute-done | bytes 1568 | tf_op jit(solution)/shard_map/ppermute | solution.py:357
  79.5 0.6 add.3
  80.1 0.0 collective-permute-done.5.rest_2_
  80.1 0.0 collective-permute-done.4.rest_1_
  80.1 1.4 %shard_map.112.sums_ref = f32[2,2,256,256]{3,2,1,0:T(8,128)S(1)} custom-call(bf16[512,384]{1,0:T(8,128)(2,1)S(1)} %get-tuple-element.22.rest_0_.own_ref, bf16[272,384]{1,0:T(8,128)(2,1)S(1)} %get-tuple-element.29.rest_0_, bf16[272,384]{1,0:T(8,128)(2,1)S(1)} %collective-permute-done.4.rest_1_, bf16[272,384]{1,0:T(8,128)(2,1)S(1)} %collective-permute-done.5.rest_2_), custom_call_target="tpu_custom_call" | custom-call | flops 1342177280 | bytes 4194304 | tf_op jit(solution)/shard_map/pallas_call | solution.py:358
  81.5 0.0 collective-permute-done.7.rest_1_
  81.5 0.0 collective-permute-done.6.rest_0_
  81.5 1.8 %shard_map.113 = (bf16[256,384]{1,0:T(8,128)(2,1)}, bf16[256,384]{1,0:T(8,128)(2,1)}) custom-call(bf16[512,384]{1,0:T(8,128)(2,1)S(1)} %get-tuple-element.22.rest_0_.own_ref, f32[2,2,256,256]{3,2,1,0:T(8,128)S(1)} %shard_map.112.sums_ref, bf16[272,384]{1,0:T(8,128)(2,1)S(1)} %collective-permute-done.6.rest_0_, ...), custom_call_target="tpu_custom_call" | custom-call | flops 1342177280 | bytes 4194304 | tf_op jit(solution)/shard_map/pallas_call | solution.py:361
  (1 shorter events, 0.0 us)
Async XLA Ops:
  1.8 12.9 %collective-permute-start.2 = (bf16[512,384]{1,0:T(8,128)(2,1)S(1)}, bf16[512,384]{1,0:T(8,128)(2,1)S(1)}, u32[]{:S(2)}, u32[]{:S(2)}) collective-permute-start(bf16[512,384]{1,0:T(8,128)(2,1)S(1)} %get-tuple-element.22.rest_0_.own_ref), channel_id=1, source_target_pairs={{16,0},{24,8},{32,16},{40,24},{48,32},{56,40},{64,48},{72,56},{80,... | collective-permute-start | bytes 1179656 | tf_op jit(solution)/shard_map/ppermute | solution.py:29
  3.1 12.8 %collective-permute-start.1 = (bf16[512,384]{1,0:T(8,128)(2,1)S(1)}, bf16[512,384]{1,0:T(8,128)(2,1)S(1)}, u32[]{:S(2)}, u32[]{:S(2)}) collective-permute-start(bf16[512,384]{1,0:T(8,128)(2,1)S(1)} %get-tuple-element.22.rest_0_.own_ref), channel_id=1, source_target_pairs={{0,16},{8,24},{16,32},{24,40},{32,48},{40,56},{48,64},{56,72},{64,... | collective-permute-start | bytes 1179656 | tf_op jit(solution)/shard_map/ppermute | solution.py:29
  7.7 11.5 %collective-permute-start = (bf16[512,384]{1,0:T(8,128)(2,1)S(1)}, bf16[512,384]{1,0:T(8,128)(2,1)S(1)}, u32[]{:S(2)}, u32[]{:S(2)}) collective-permute-start(bf16[512,384]{1,0:T(8,128)(2,1)S(1)} %get-tuple-element.22.rest_0_.own_ref), channel_id=1, source_target_pairs={{0,8},{8,0},{16,24},{24,16},{32,40},{40,32},{48,56},{56,48},{64,72... | collective-permute-start | bytes 1179656 | tf_op jit(solution)/shard_map/ppermute | solution.py:29
  16.0 3.6 %collective-permute-start.3 = (bf16[512,384]{1,0:T(8,128)(2,1)S(1)}, bf16[512,384]{1,0:T(8,128)(2,1)S(1)}, u32[]{:S(2)}, u32[]{:S(2)}) collective-permute-start(bf16[512,384]{1,0:T(8,128)(2,1)S(1)} %broadcast_select_fusion), channel_id=1, source_target_pairs={{0,8},{8,0},{16,24},{24,16},{32,40},{40,32},{48,56},{56,48},{64,72... | collective-permute-start | bytes 1179656 | tf_op jit(solution)/shard_map/ppermute | solution.py:29
  37.5 42.6 %collective-permute-start.5 = (bf16[272,384]{1,0:T(8,128)(2,1)S(1)}, bf16[272,384]{1,0:T(8,128)(2,1)S(1)}, u32[]{:S(2)}, u32[]{:S(2)}) collective-permute-start(bf16[272,384]{1,0:T(8,128)(2,1)S(1)} %get-tuple-element.29.rest_0_), channel_id=1, source_target_pairs={{0,16},{8,24},{16,32},{24,40},{32,48},{40,56},{48,64},{56,72},{64,... | collective-permute-start | bytes 626696 | tf_op jit(solution)/shard_map/ppermute | solution.py:29
  41.9 38.2 %collective-permute-start.4 = (bf16[272,384]{1,0:T(8,128)(2,1)S(1)}, bf16[272,384]{1,0:T(8,128)(2,1)S(1)}, u32[]{:S(2)}, u32[]{:S(2)}) collective-permute-start(bf16[272,384]{1,0:T(8,128)(2,1)S(1)} %get-tuple-element.29.rest_0_), channel_id=1, source_target_pairs={{0,8},{8,0},{16,24},{24,16},{32,40},{40,32},{48,56},{56,48},{64,72... | collective-permute-start | bytes 626696 | tf_op jit(solution)/shard_map/ppermute | solution.py:29
  43.8 30.2 %all-to-all-start.1 = ((f32[32,1,384]{2,1,0:T(1,128)}), f32[32,1,384]{2,1,0:T(1,128)S(1)}, u32[]{:S(2)}, u32[]{:S(2)}) async-start(f32[32,1,384]{2,1,0:T(1,128)} %get-tuple-element.32), calls=%async_computation.1 | async-start | bytes 98304 | tf_op jit(solution)/shard_map/all_to_all | solution.py:348
  60.3 21.2 %collective-permute-start.7 = (bf16[272,384]{1,0:T(8,128)(2,1)S(1)}, bf16[272,384]{1,0:T(8,128)(2,1)S(1)}, u32[]{:S(2)}, u32[]{:S(2)}) collective-permute-start(bf16[272,384]{1,0:T(8,128)(2,1)S(1)} %get-tuple-element.29.rest_0_), channel_id=1, source_target_pairs={{8,16},{16,8},{24,32},{32,24},{40,48},{48,40},{56,64},{64,56},{72,... | collective-permute-start | bytes 626696 | tf_op jit(solution)/shard_map/ppermute | solution.py:29
  61.0 20.5 %collective-permute-start.6 = (bf16[272,384]{1,0:T(8,128)(2,1)S(1)}, bf16[272,384]{1,0:T(8,128)(2,1)S(1)}, u32[]{:S(2)}, u32[]{:S(2)}) collective-permute-start(bf16[272,384]{1,0:T(8,128)(2,1)S(1)} %get-tuple-element.29.rest_0_), channel_id=1, source_target_pairs={{16,0},{24,8},{32,16},{40,24},{48,32},{56,40},{64,48},{72,56},{80,... | collective-permute-start | bytes 626696 | tf_op jit(solution)/shard_map/ppermute | solution.py:29
  74.0 5.5 %collective-permute-start.8 = (f32[384]{0:T(512)S(1)}, f32[384]{0:T(512)S(1)}, u32[]{:S(2)}, u32[]{:S(2)}) collective-permute-start(f32[384]{0:T(512)S(1)} %reduce_sum.9), channel_id=1, source_target_pairs={{0,256},{256,0},{1,257},{257,1},{2,258},{258,2},{3,259},{259,3},{4... | collective-permute-start | bytes 4616 | tf_op jit(solution)/shard_map/ppermute | solution.py:357

commit v4 on v2

--- a/solution.py
+++ b/solution.py
@@ -157,11 +157,7 @@
         stats_ref[index] = stats[8:10]
 
 
-def token_kernel(
-    start_ref, end_ref, q_ref, go_ref, gain_ref, attn_ref, probs_ref, norms_ref, stats_ref, *rest
-):
-    pieces = rest[:PIECES]
-    attended_ref, gain_part_ref, gq_ref, sent_ref, grads = rest[PIECES:]
+def norm_kernel(go_ref, gain_ref, attn_ref, stats_ref, attended_ref, gain_part_ref, cot_ref):
     stats = stats_ref[0]
     for index in range(1, TENSOR):
         stats = stats + stats_ref[index]
@@ -173,13 +169,16 @@
     gain = gain_ref[...]
     normed = attn_ref[...] * inv
     attended_ref[...] = (normed * gain).astype(jnp.bfloat16)
-    gain_part_ref[...] = jnp.broadcast_to(
-        jnp.sum(grad * normed, axis=0, keepdims=True)[None], (SEQ, 1, W)
-    )
-    grad_attn = (inv * (grad * gain - normed * mean_cross)).astype(jnp.bfloat16)
-    rows = q_ref[...]
+    gain_part_ref[...] = jnp.sum(grad * normed, axis=0, keepdims=True)
+    cot_ref[...] = (inv * (grad * gain - normed * mean_cross)).astype(jnp.bfloat16)
+
+
+def token_kernel(start_ref, end_ref, q_ref, cot_ref, probs_ref, norms_ref, *rest):
+    pieces = rest[:PIECES]
+    gq_ref, sent_ref, grads = rest[PIECES:]
+    grad_attn = cot_ref[...]
     sent_ref[0:TB] = grad_attn
-    sent_ref[TB : 2 * TB] = rows
+    sent_ref[TB : 2 * TB] = q_ref[...]
     grad_q = []
     inners = []
     for pair in range(2):
@@ -216,19 +215,20 @@
     )
 
 
-def frame_kernel(own_ref, *rest):
-    tokens = rest[:PIECES]
-    gk_ref, gv_ref = rest[PIECES:]
+def spread_kernel(mine_ref, other_ref, out_ref):
+    out_ref[...] = jnp.broadcast_to((mine_ref[...] + other_ref[...])[None], (SEQ, 1, W))
+
+
+def frame_sums(own_ref, tokens):
     here = lax.axis_index("seq")
     totals = []
-    extras = [merge(tokens[index][2 * TB : 2 * TB + 16]) for index in range(PIECES)]
+    extras = [merge(token[2 * TB : 2 * TB + 16]) for token in tokens]
     for pair in range(2):
         at = PAIRS[pair][0]
         keys = own_ref[0:FR, at : at + 256]
         values = own_ref[FR : 2 * FR, at : at + 256]
-        grad_k = None
-        for index in range(PIECES):
-            extra = extras[index]
+        grad_k = grad_v = None
+        for index, extra in enumerate(extras):
 
             def both(base):
                 low = base + 2 * pair
@@ -260,9 +260,16 @@
                 grad_k, grad_v = part_k, part_v
             else:
                 grad_k, grad_v = grad_k + part_k, grad_v + part_v
-        totals.append((grad_k * SCALE, grad_v))
-    for which, out in ((0, gk_ref), (1, gv_ref)):
-        low, high = totals[0][which], totals[1][which]
+        totals.append((grad_k, grad_v))
+    return totals
+
+
+def frame_kernel(own_ref, *rest):
+    tokens = rest[:PIECES]
+    outs = rest[PIECES:]
+    totals = frame_sums(own_ref, tokens)
+    for which, (out, scale) in enumerate(zip(outs, (SCALE, 1.0))):
+        low, high = totals[0][which] * scale, totals[1][which] * scale
         out[:, 0:128] = low[:, :128].astype(out.dtype)
         out[:, 128:256] = (low[:, 128:] + high[:, :128]).astype(out.dtype)
         out[:, 256:384] = high[:, 128:].astype(out.dtype)
@@ -324,14 +331,20 @@
         vectors=3 + PIECES,
     )(band_start, band_end, query, grad, gain_row, *pieces)
     stats = lax.all_to_all(stats, "tensor", 0, 0, tiled=False)
-    attended, gain_part, grad_queries, sent = call(
+    attended, gain_part, cot = call(
+        norm_kernel, (((TB, W), bf16), ((1, W), f32), ((TB, W), bf16)), 0, vectors=4
+    )(grad, gain_row, attn, stats)
+    gain_other = lax.ppermute(gain_part, "dp", [(0, 1), (1, 0)])
+    grad_queries, sent = call(
         token_kernel,
-        (((TB, W), bf16), ((SEQ, 1, W), f32), ((TB, W), bf16), ((2 * TB + 16, W), bf16)),
+        (((TB, W), bf16), ((2 * TB + 16, W), bf16)),
         2,
         scratch=(whole,),
         scalars=2,
-        vectors=7 + PIECES,
-    )(band_start, band_end, query, grad, gain_row, attn, probs, norms, stats, *pieces)
+        vectors=4 + PIECES,
+    )(band_start, band_end, query, cot, probs, norms, *pieces)
+    (gain_both,) = call(spread_kernel, (((SEQ, 1, W), f32),), 0, vectors=2)(gain_part, gain_other)
+    spread = lax.all_to_all(gain_both, "seq", 0, 0, tiled=False)
     tokens = (
         sent,
         permute(sent, "seq", lambda i: i ^ 1),
@@ -339,12 +352,10 @@
         permute(sent, "seq", lambda i: i - 2),
         permute(sent, "seq", lambda i: i - 1 if i % 2 == 0 else i + 1),
     )
-    gain_sum = jnp.sum(lax.all_to_all(gain_part, "seq", 0, 0, tiled=False), axis=(0, 1))
-    gain_other = lax.ppermute(gain_sum, "dp", [(0, 1), (1, 0)])
     grad_keys, grad_values = call(
         frame_kernel, (((FR, W), bf16), ((FR, W), bf16)), 4, vectors=1 + PIECES
     )(own, *tokens)
-    grad_gain = gain_sum + gain_other
+    grad_gain = jnp.sum(spread, axis=(0, 1))
     return (
         attended[None],
         grad_queries[None],

time: 89.8 us -> 91.3 us (1.017)
  the two profiles are of different devices: /device:TPU:2 before, /device:TPU:1 now
where the time goes in v4:
time: 91.3 us; the launch traced here: 90.8 us
  blocking collectives  41.6 us (46%)
  starting transfers between devices  35.2 us (39%)
  Pallas kernels  9.09 us (10%)
  waiting for transfers between devices  2.14 us (2%)
  between operations  2.06 us (2%)
    ppermute x8, starting transfers between devices, permute(): return lax.ppermute(array, axis, pairs)  33 us
    all_to_all x1, blocking collectives, per_device(): spread = lax.all_to_all(gain_both, 'seq', 0, 0, tiled=False)  31 us
    all_to_all x1, blocking collectives, per_device(): stats = lax.all_to_all(stats, 'tensor', 0, 0, tiled=False)  10.6 us
    pallas_call x1, Pallas kernels, per_device(): call(frame_kernel, (((FR, W), bf16), ((FR, W), bf16)), 4, vectors=1 + PIE...  3.01 us
    ppermute x1, starting transfers between devices, per_device(): gain_other = lax.ppermute(gain_part, 'dp', [(0, 1), (1, 0)])  2.22 us
    pallas_call x1, Pallas kernels, per_device(): call(token_kernel, (((TB, W), bf16), ((2 * TB + 16, W), bf16)), 2, scratc...  2.13 us
    ppermute x1, waiting for transfers between devices, per_device(): gain_other = lax.ppermute(gain_part, 'dp', [(0, 1), (1, 0)])  2.1 us
    pallas_call x1, Pallas kernels, per_device(): call(forward_kernel, (((TB, W), f32), ((2, *whole), f32), ((TENSOR, 2, TB...  1.91 us
  transfers between devices with their start and end apart: 9, of which 1 were waited for; matrix products, arithmetic and copies ran while one was open for 1% of the time, Pallas kernels for 0%

profile of v4, /device:TPU:1, one launch (start us, length us, event | category | flops | bytes accessed | tf_op | source)
XLA Modules:
  0.0 90.8 jit_solution(9705841972177734740)
XLA Ops:
  0.6 1.2 %pack.1 = (bf16[512,384]{1,0:T(8,128)(2,1)S(1)}, bf16[128,384]{1,0:T(8,128)(2,1)S(1)}, bf16[128,384]{1,0:T(8,128)(2,1)S(1)}, f32[1,384]{1,0:T(1,128)S(1)}) custom-call(bf16[256,384]{1,0:T(8,128)(2,1)} %bitcast.8, bf16[256,384]{1,0:T(8,128)(2,1)} %bitcast.9, bf16[128,384]{1,0:T(8,128)(2,1)} %bitcast.10, bf16[128,384]{1,0:T(8,128)(2,1)} %bitcast.11, f32[384]{0:T(512)} %gain_ref.1), custom_call_target="tpu_custom_call" | custom-call | tf_op jit(solution)/shard_map/pack/pallas_call | solution.py:302
  1.8 1.3 %collective-permute-start.2 = (bf16[512,384]{1,0:T(8,128)(2,1)S(1)}, bf16[512,384]{1,0:T(8,128)(2,1)S(1)}, u32[]{:S(2)}, u32[]{:S(2)}) collective-permute-start(bf16[512,384]{1,0:T(8,128)(2,1)S(1)} %get-tuple-element.23.rest_0_.own_ref), channel_id=1, source_target_pairs={{16,0},{24,8},{32,16},{40,24},{48,32},{56,40},{64,48},{72,56},{80,... | collective-permute-start | bytes 1179656 | tf_op jit(solution)/shard_map/ppermute | solution.py:28
  3.1 5.0 %collective-permute-start.1 = (bf16[512,384]{1,0:T(8,128)(2,1)S(1)}, bf16[512,384]{1,0:T(8,128)(2,1)S(1)}, u32[]{:S(2)}, u32[]{:S(2)}) collective-permute-start(bf16[512,384]{1,0:T(8,128)(2,1)S(1)} %get-tuple-element.23.rest_0_.own_ref), channel_id=1, source_target_pairs={{0,16},{8,24},{16,32},{24,40},{32,48},{40,56},{48,64},{56,72},{64,... | collective-permute-start | bytes 1179656 | tf_op jit(solution)/shard_map/ppermute | solution.py:28
  8.1 8.3 %collective-permute-start = (bf16[512,384]{1,0:T(8,128)(2,1)S(1)}, bf16[512,384]{1,0:T(8,128)(2,1)S(1)}, u32[]{:S(2)}, u32[]{:S(2)}) collective-permute-start(bf16[512,384]{1,0:T(8,128)(2,1)S(1)} %get-tuple-element.23.rest_0_.own_ref), channel_id=1, source_target_pairs={{0,8},{8,0},{16,24},{24,16},{32,40},{40,32},{48,56},{56,48},{64,72... | collective-permute-start | bytes 1179656 | tf_op jit(solution)/shard_map/ppermute | solution.py:28
  16.5 0.0 collective-permute-done.2.rest_3_
  16.5 0.0 collective-permute-done.1.rest_2_
  16.5 0.1 broadcast_select_fusion
  16.5 5.2 %collective-permute-start.3 = (bf16[512,384]{1,0:T(8,128)(2,1)S(1)}, bf16[512,384]{1,0:T(8,128)(2,1)S(1)}, u32[]{:S(2)}, u32[]{:S(2)}) collective-permute-start(bf16[512,384]{1,0:T(8,128)(2,1)S(1)} %broadcast_select_fusion), channel_id=1, source_target_pairs={{0,8},{8,0},{16,24},{24,16},{32,40},{40,32},{48,56},{56,48},{64,72... | collective-permute-start | bytes 1179656 | tf_op jit(solution)/shard_map/ppermute | solution.py:28
  23.1 0.0 collective-permute-done.rest_1_
  23.1 0.0 collective-permute-done.3.rest_4_
  23.1 1.9 %shard_map.110 = (f32[128,384]{1,0:T(8,128)S(1)}, f32[2,256,1280]{2,1,0:T(8,128)S(1)}, f32[8,2,128]{2,1,0:T(2,128)S(1)}, f32[8,128]{1,0:T(8,128)S(1)}) custom-call(s32[1,1]{1,0:T(1,128)S(6)} %copy.12.start_ref, s32[1,1]{1,0:T(1,128)S(6)} %copy.13.end_ref, bf16[128,384]{1,0:T(8,128)(2,1)S(1)} %get-tuple-element.22.q_ref, ...), custom_call_target="tpu_custom_call" | custom-call | flops 671088640 | bytes 4194304 | tf_op jit(solution)/shard_map/pallas_call | solution.py:325
  25.0 10.6 %all_to_all.10.stats_ref = f32[8,2,128]{2,1,0:T(2,128)S(1)} all-to-all(f32[8,2,128]{2,1,0:T(2,128)S(1)} %get-tuple-element.25), channel_id=1, replica_groups=mesh['dp'=2,'seq'=32,'tensor'=8] {'tensor'}, dimensions={0} | all-to-all | bytes 16384 | tf_op jit(solution)/shard_map/all_to_all | solution.py:333
  35.6 0.9 shard_map.111
  36.5 2.1 %shard_map.112 = (bf16[128,384]{1,0:T(8,128)(2,1)}, bf16[272,384]{1,0:T(8,128)(2,1)S(1)}) custom-call(s32[1,1]{1,0:T(1,128)S(6)} %copy.12.start_ref, s32[1,1]{1,0:T(1,128)S(6)} %copy.13.end_ref, bf16[128,384]{1,0:T(8,128)(2,1)S(1)} %get-tuple-element.22.q_ref, bf16[128,384]{1,0:T(8,128)(2,1)S(1)} %get-tuple-element.27.cot_ref, ...), custom_call_target="tpu_custom_call" | custom-call | flops 671088640 | bytes 4194304 | tf_op jit(solution)/shard_map/pallas_call | solution.py:338
  38.6 5.8 %collective-permute-start.7 = (bf16[272,384]{1,0:T(8,128)(2,1)S(1)}, bf16[272,384]{1,0:T(8,128)(2,1)S(1)}, u32[]{:S(2)}, u32[]{:S(2)}) collective-permute-start(bf16[272,384]{1,0:T(8,128)(2,1)S(1)} %get-tuple-element.31.rest_0_), channel_id=1, source_target_pairs={{8,16},{16,8},{24,32},{32,24},{40,48},{48,40},{56,64},{64,56},{72,... | collective-permute-start | bytes 626696 | tf_op jit(solution)/shard_map/ppermute | solution.py:28
  44.4 1.3 %collective-permute-start.6 = (bf16[272,384]{1,0:T(8,128)(2,1)S(1)}, bf16[272,384]{1,0:T(8,128)(2,1)S(1)}, u32[]{:S(2)}, u32[]{:S(2)}) collective-permute-start(bf16[272,384]{1,0:T(8,128)(2,1)S(1)} %get-tuple-element.31.rest_0_), channel_id=1, source_target_pairs={{16,0},{24,8},{32,16},{40,24},{48,32},{56,40},{64,48},{72,56},{80,... | collective-permute-start | bytes 626696 | tf_op jit(solution)/shard_map/ppermute | solution.py:28
  45.7 4.2 %collective-permute-start.5 = (bf16[272,384]{1,0:T(8,128)(2,1)S(1)}, bf16[272,384]{1,0:T(8,128)(2,1)S(1)}, u32[]{:S(2)}, u32[]{:S(2)}) collective-permute-start(bf16[272,384]{1,0:T(8,128)(2,1)S(1)} %get-tuple-element.31.rest_0_), channel_id=1, source_target_pairs={{0,16},{8,24},{16,32},{24,40},{32,48},{40,56},{48,64},{56,72},{64,... | collective-permute-start | bytes 626696 | tf_op jit(solution)/shard_map/ppermute | solution.py:28
  49.9 1.9 %collective-permute-start.4 = (bf16[272,384]{1,0:T(8,128)(2,1)S(1)}, bf16[272,384]{1,0:T(8,128)(2,1)S(1)}, u32[]{:S(2)}, u32[]{:S(2)}) collective-permute-start(bf16[272,384]{1,0:T(8,128)(2,1)S(1)} %get-tuple-element.31.rest_0_), channel_id=1, source_target_pairs={{0,8},{8,0},{16,24},{24,16},{32,40},{40,32},{48,56},{56,48},{64,72... | collective-permute-start | bytes 626696 | tf_op jit(solution)/shard_map/ppermute | solution.py:28
  51.8 2.2 %collective-permute-start.8 = (f32[1,384]{1,0:T(1,128)S(1)}, f32[1,384]{1,0:T(1,128)S(1)}, u32[]{:S(2)}, u32[]{:S(2)}) collective-permute-start(f32[1,384]{1,0:T(1,128)S(1)} %get-tuple-element.34.mine_ref), channel_id=1, source_target_pairs={{0,256},{256,0},{1,257},{257,1},{2,258},{258,2},{3,259},{259,3},{4... | collective-permute-start | bytes 4616 | tf_op jit(solution)/shard_map/ppermute | solution.py:337
  54.0 2.1 %collective-permute-done.8.other_ref = f32[1,384]{1,0:T(1,128)S(1)} collective-permute-done((f32[1,384]{1,0:T(1,128)S(1)}, f32[1,384]{1,0:T(1,128)S(1)}, u32[]{:S(2)}, u32[]{:S(2)}) %collective-permute-start.8) | collective-permute-done | bytes 1568 | tf_op jit(solution)/shard_map/ppermute | solution.py:337
  56.2 31.0 %all_to_all.11 = f32[32,1,384]{2,1,0:T(1,128)S(1)} all-to-all(f32[32,1,384]{2,1,0:T(1,128)S(1)} %shard_map.114), channel_id=1, replica_groups=mesh['dp'=2,'seq'=32,'tensor'=8] {'seq'}, dimensions={0} | all-to-all | bytes 98304 | tf_op jit(solution)/shard_map/all_to_all | solution.py:347
  87.2 0.6 reduce_sum.9
  87.8 0.0 collective-permute-done.7.rest_4_
  87.8 0.0 collective-permute-done.6.rest_3_
  87.8 0.0 collective-permute-done.5.rest_2_
  87.8 0.0 collective-permute-done.4.rest_1_
  87.8 3.0 %shard_map.113 = (bf16[256,384]{1,0:T(8,128)(2,1)}, bf16[256,384]{1,0:T(8,128)(2,1)}) custom-call(bf16[512,384]{1,0:T(8,128)(2,1)S(1)} %get-tuple-element.23.rest_0_.own_ref, bf16[272,384]{1,0:T(8,128)(2,1)S(1)} %get-tuple-element.31.rest_0_, bf16[272,384]{1,0:T(8,128)(2,1)S(1)} %collective-permute-done.4.rest_1_, ...), custom_call_target="tpu_custom_call" | custom-call | flops 1342177280 | bytes 4194304 | tf_op jit(solution)/shard_map/pallas_call | solution.py:355
  (1 shorter events, 0.0 us)
Async XLA Ops:
  1.8 14.6 %collective-permute-start.2 = (bf16[512,384]{1,0:T(8,128)(2,1)S(1)}, bf16[512,384]{1,0:T(8,128)(2,1)S(1)}, u32[]{:S(2)}, u32[]{:S(2)}) collective-permute-start(bf16[512,384]{1,0:T(8,128)(2,1)S(1)} %get-tuple-element.23.rest_0_.own_ref), channel_id=1, source_target_pairs={{16,0},{24,8},{32,16},{40,24},{48,32},{56,40},{64,48},{72,56},{80,... | collective-permute-start | bytes 1179656 | tf_op jit(solution)/shard_map/ppermute | solution.py:28
  3.1 13.4 %collective-permute-start.1 = (bf16[512,384]{1,0:T(8,128)(2,1)S(1)}, bf16[512,384]{1,0:T(8,128)(2,1)S(1)}, u32[]{:S(2)}, u32[]{:S(2)}) collective-permute-start(bf16[512,384]{1,0:T(8,128)(2,1)S(1)} %get-tuple-element.23.rest_0_.own_ref), channel_id=1, source_target_pairs={{0,16},{8,24},{16,32},{24,40},{32,48},{40,56},{48,64},{56,72},{64,... | collective-permute-start | bytes 1179656 | tf_op jit(solution)/shard_map/ppermute | solution.py:28
  8.1 14.9 %collective-permute-start = (bf16[512,384]{1,0:T(8,128)(2,1)S(1)}, bf16[512,384]{1,0:T(8,128)(2,1)S(1)}, u32[]{:S(2)}, u32[]{:S(2)}) collective-permute-start(bf16[512,384]{1,0:T(8,128)(2,1)S(1)} %get-tuple-element.23.rest_0_.own_ref), channel_id=1, source_target_pairs={{0,8},{8,0},{16,24},{24,16},{32,40},{40,32},{48,56},{56,48},{64,72... | collective-permute-start | bytes 1179656 | tf_op jit(solution)/shard_map/ppermute | solution.py:28
  16.5 6.5 %collective-permute-start.3 = (bf16[512,384]{1,0:T(8,128)(2,1)S(1)}, bf16[512,384]{1,0:T(8,128)(2,1)S(1)}, u32[]{:S(2)}, u32[]{:S(2)}) collective-permute-start(bf16[512,384]{1,0:T(8,128)(2,1)S(1)} %broadcast_select_fusion), channel_id=1, source_target_pairs={{0,8},{8,0},{16,24},{24,16},{32,40},{40,32},{48,56},{56,48},{64,72... | collective-permute-start | bytes 1179656 | tf_op jit(solution)/shard_map/ppermute | solution.py:28
  38.6 49.2 %collective-permute-start.7 = (bf16[272,384]{1,0:T(8,128)(2,1)S(1)}, bf16[272,384]{1,0:T(8,128)(2,1)S(1)}, u32[]{:S(2)}, u32[]{:S(2)}) collective-permute-start(bf16[272,384]{1,0:T(8,128)(2,1)S(1)} %get-tuple-element.31.rest_0_), channel_id=1, source_target_pairs={{8,16},{16,8},{24,32},{32,24},{40,48},{48,40},{56,64},{64,56},{72,... | collective-permute-start | bytes 626696 | tf_op jit(solution)/shard_map/ppermute | solution.py:28
  44.4 43.4 %collective-permute-start.6 = (bf16[272,384]{1,0:T(8,128)(2,1)S(1)}, bf16[272,384]{1,0:T(8,128)(2,1)S(1)}, u32[]{:S(2)}, u32[]{:S(2)}) collective-permute-start(bf16[272,384]{1,0:T(8,128)(2,1)S(1)} %get-tuple-element.31.rest_0_), channel_id=1, source_target_pairs={{16,0},{24,8},{32,16},{40,24},{48,32},{56,40},{64,48},{72,56},{80,... | collective-permute-start | bytes 626696 | tf_op jit(solution)/shard_map/ppermute | solution.py:28
  45.7 42.1 %collective-permute-start.5 = (bf16[272,384]{1,0:T(8,128)(2,1)S(1)}, bf16[272,384]{1,0:T(8,128)(2,1)S(1)}, u32[]{:S(2)}, u32[]{:S(2)}) collective-permute-start(bf16[272,384]{1,0:T(8,128)(2,1)S(1)} %get-tuple-element.31.rest_0_), channel_id=1, source_target_pairs={{0,16},{8,24},{16,32},{24,40},{32,48},{40,56},{48,64},{56,72},{64,... | collective-permute-start | bytes 626696 | tf_op jit(solution)/shard_map/ppermute | solution.py:28
  49.9 37.9 %collective-permute-start.4 = (bf16[272,384]{1,0:T(8,128)(2,1)S(1)}, bf16[272,384]{1,0:T(8,128)(2,1)S(1)}, u32[]{:S(2)}, u32[]{:S(2)}) collective-permute-start(bf16[272,384]{1,0:T(8,128)(2,1)S(1)} %get-tuple-element.31.rest_0_), channel_id=1, source_target_pairs={{0,8},{8,0},{16,24},{24,16},{32,40},{40,32},{48,56},{56,48},{64,72... | collective-permute-start | bytes 626696 | tf_op jit(solution)/shard_map/ppermute | solution.py:28
  51.8 4.3 %collective-permute-start.8 = (f32[1,384]{1,0:T(1,128)S(1)}, f32[1,384]{1,0:T(1,128)S(1)}, u32[]{:S(2)}, u32[]{:S(2)}) collective-permute-start(f32[1,384]{1,0:T(1,128)S(1)} %get-tuple-element.34.mine_ref), channel_id=1, source_target_pairs={{0,256},{256,0},{1,257},{257,1},{2,258},{258,2},{3,259},{259,3},{4... | collective-permute-start | bytes 4616 | tf_op jit(solution)/shard_map/ppermute | solution.py:337

commit v5 on v2

--- a/solution.py
+++ b/solution.py
@@ -216,19 +216,15 @@
     )
 
 
-def frame_kernel(own_ref, *rest):
-    tokens = rest[:PIECES]
-    gk_ref, gv_ref = rest[PIECES:]
-    here = lax.axis_index("seq")
+def frame_sums(kv_ref, here, tokens):
     totals = []
-    extras = [merge(tokens[index][2 * TB : 2 * TB + 16]) for index in range(PIECES)]
+    extras = [merge(token[2 * TB : 2 * TB + 16]) for token in tokens]
     for pair in range(2):
         at = PAIRS[pair][0]
-        keys = own_ref[0:FR, at : at + 256]
-        values = own_ref[FR : 2 * FR, at : at + 256]
-        grad_k = None
-        for index in range(PIECES):
-            extra = extras[index]
+        keys = kv_ref[0:FR, at : at + 256]
+        values = kv_ref[FR : 2 * FR, at : at + 256]
+        grad_k = grad_v = None
+        for index, extra in enumerate(extras):
 
             def both(base):
                 low = base + 2 * pair
@@ -260,12 +256,32 @@
                 grad_k, grad_v = part_k, part_v
             else:
                 grad_k, grad_v = grad_k + part_k, grad_v + part_v
-        totals.append((grad_k * SCALE, grad_v))
-    for which, out in ((0, gk_ref), (1, gv_ref)):
-        low, high = totals[0][which], totals[1][which]
-        out[:, 0:128] = low[:, :128].astype(out.dtype)
-        out[:, 128:256] = (low[:, 128:] + high[:, :128]).astype(out.dtype)
-        out[:, 256:384] = high[:, 128:].astype(out.dtype)
+        totals.append((grad_k, grad_v))
+    return totals
+
+
+def columns(totals, which):
+    low, high = totals[0][which], totals[1][which]
+    return ((0, low[:, :128]), (128, low[:, 128:] + high[:, :128]), (256, high[:, 128:]))
+
+
+def partner_frame_kernel(kv_ref, sent_ref, below_ref, above_ref, out_ref):
+    here = lax.axis_index("seq")
+    core = lax.rem(here, 2)
+    far = jnp.where(core == 0, above_ref[...], below_ref[...])
+    totals = frame_sums(kv_ref, here + 1 - 2 * core, (sent_ref[...], far))
+    for which in range(2):
+        for at, part in columns(totals, which):
+            out_ref[which * FR : (which + 1) * FR, at : at + 128] = part.astype(out_ref.dtype)
+
+
+def own_frame_kernel(kv_ref, sent_ref, below_ref, above_ref, more_ref, gk_ref, gv_ref):
+    tokens = (sent_ref[...], below_ref[...], above_ref[...])
+    totals = frame_sums(kv_ref, lax.axis_index("seq"), tokens)
+    for which, (out, scale) in enumerate(((gk_ref, SCALE), (gv_ref, 1.0))):
+        for at, part in columns(totals, which):
+            more = more_ref[which * FR : (which + 1) * FR, at : at + 128].astype(jnp.float32)
+            out[:, at : at + 128] = ((part + more) * scale).astype(out.dtype)
 
 
 VMEM = pl.BlockSpec(memory_space=pltpu.VMEM)
@@ -332,18 +348,17 @@
         scalars=2,
         vectors=7 + PIECES,
     )(band_start, band_end, query, grad, gain_row, attn, probs, norms, stats, *pieces)
-    tokens = (
-        sent,
-        permute(sent, "seq", lambda i: i ^ 1),
-        permute(sent, "seq", lambda i: i + 2),
-        permute(sent, "seq", lambda i: i - 2),
-        permute(sent, "seq", lambda i: i - 1 if i % 2 == 0 else i + 1),
-    )
-    gain_sum = jnp.sum(lax.all_to_all(gain_part, "seq", 0, 0, tiled=False), axis=(0, 1))
+    spread = lax.all_to_all(gain_part, "seq", 0, 0, tiled=False)
+    gain_sum = jnp.sum(spread, axis=(0, 1))
+    tokens = (sent, permute(sent, "seq", lambda i: i + 2), permute(sent, "seq", lambda i: i - 2))
+    (to_partner,) = call(
+        partner_frame_kernel, (((2 * FR, W), bf16),), 2, vectors=4
+    )(partner, *tokens)
+    from_partner = permute(to_partner, "seq", lambda i: i ^ 1)
     gain_other = lax.ppermute(gain_sum, "dp", [(0, 1), (1, 0)])
     grad_keys, grad_values = call(
-        frame_kernel, (((FR, W), bf16), ((FR, W), bf16)), 4, vectors=1 + PIECES
-    )(own, *tokens)
+        own_frame_kernel, (((FR, W), bf16), ((FR, W), bf16)), 2, vectors=5
+    )(own, *tokens, from_partner)
     grad_gain = gain_sum + gain_other
     return (
         attended[None],

time: 89.8 us -> 90.7 us (1.010)
  the two profiles are of different devices: /device:TPU:2 before, /device:TPU:6 now
where the time goes in v5:
time: 90.7 us; the launch traced here: 89 us
  blocking collectives  44 us (49%)
  starting transfers between devices  20.4 us (22%)
  waiting for transfers between devices  13.2 us (15%)
  Pallas kernels  8.59 us (9%)
  between operations  2.03 us (2%)
    all_to_all x1, blocking collectives, per_device(): spread = lax.all_to_all(gain_part, 'seq', 0, 0, tiled=False)  32 us
    ppermute x7, starting transfers between devices, permute(): return lax.ppermute(array, axis, pairs)  17.9 us
    all_to_all x1, blocking collectives, per_device(): stats = lax.all_to_all(stats, 'tensor', 0, 0, tiled=False)  12 us
    ppermute x7, waiting for transfers between devices, permute(): return lax.ppermute(array, axis, pairs)  10.2 us
    ppermute x1, waiting for transfers between devices, per_device(): gain_other = lax.ppermute(gain_sum, 'dp', [(0, 1), (1, 0)])  2.99 us
    ppermute x1, starting transfers between devices, per_device(): gain_other = lax.ppermute(gain_sum, 'dp', [(0, 1), (1, 0)])  2.47 us
    pallas_call x1, Pallas kernels, per_device(): call(token_kernel, (((TB, W), bf16), ((SEQ, 1, W), f32), ((TB, W), bf16),...  2.45 us
    pallas_call x1, Pallas kernels, per_device(): call(own_frame_kernel, (((FR, W), bf16), ((FR, W), bf16)), 2, vectors=5)  2.12 us
  transfers between devices with their start and end apart: 8, of which 6 were waited for; matrix products, arithmetic and copies ran while one was open for 1% of the time, Pallas kernels for 0%

profile of v5, /device:TPU:6, one launch (start us, length us, event | category | flops | bytes accessed | tf_op | source)
XLA Modules:
  0.0 89.0 jit_solution(3115323582362718128)
XLA Ops:
  0.6 1.2 %pack.1 = (bf16[512,384]{1,0:T(8,128)(2,1)S(1)}, bf16[128,384]{1,0:T(8,128)(2,1)S(1)}, bf16[128,384]{1,0:T(8,128)(2,1)S(1)}, f32[1,384]{1,0:T(1,128)S(1)}) custom-call(bf16[256,384]{1,0:T(8,128)(2,1)} %bitcast.8, bf16[256,384]{1,0:T(8,128)(2,1)} %bitcast.9, bf16[128,384]{1,0:T(8,128)(2,1)} %bitcast.10, bf16[128,384]{1,0:T(8,128)(2,1)} %bitcast.11, f32[384]{0:T(512)} %gain_ref.1), custom_call_target="tpu_custom_call" | custom-call | tf_op jit(solution)/shard_map/pack/pallas_call | solution.py:311
  1.8 1.3 %collective-permute-start.2 = (bf16[512,384]{1,0:T(8,128)(2,1)S(1)}, bf16[512,384]{1,0:T(8,128)(2,1)S(1)}, u32[]{:S(2)}, u32[]{:S(2)}) collective-permute-start(bf16[512,384]{1,0:T(8,128)(2,1)S(1)} %get-tuple-element.22.rest_0_.kv_ref), channel_id=1, source_target_pairs={{16,0},{24,8},{32,16},{40,24},{48,32},{56,40},{64,48},{72,56},{80,... | collective-permute-start | bytes 1179656 | tf_op jit(solution)/shard_map/ppermute | solution.py:28
  3.1 4.6 %collective-permute-start.1 = (bf16[512,384]{1,0:T(8,128)(2,1)S(1)}, bf16[512,384]{1,0:T(8,128)(2,1)S(1)}, u32[]{:S(2)}, u32[]{:S(2)}) collective-permute-start(bf16[512,384]{1,0:T(8,128)(2,1)S(1)} %get-tuple-element.22.rest_0_.kv_ref), channel_id=1, source_target_pairs={{0,16},{8,24},{16,32},{24,40},{32,48},{40,56},{48,64},{56,72},{64,... | collective-permute-start | bytes 1179656 | tf_op jit(solution)/shard_map/ppermute | solution.py:28
  7.7 1.9 %collective-permute-start = (bf16[512,384]{1,0:T(8,128)(2,1)S(1)}, bf16[512,384]{1,0:T(8,128)(2,1)S(1)}, u32[]{:S(2)}, u32[]{:S(2)}) collective-permute-start(bf16[512,384]{1,0:T(8,128)(2,1)S(1)} %get-tuple-element.22.rest_0_.kv_ref), channel_id=1, source_target_pairs={{0,8},{8,0},{16,24},{24,16},{32,40},{40,32},{48,56},{56,48},{64,72... | collective-permute-start | bytes 1179656 | tf_op jit(solution)/shard_map/ppermute | solution.py:28
  9.6 5.1 %collective-permute-done.2.rest_3_ = bf16[512,384]{1,0:T(8,128)(2,1)S(1)} collective-permute-done((bf16[512,384]{1,0:T(8,128)(2,1)S(1)}, bf16[512,384]{1,0:T(8,128)(2,1)S(1)}, u32[]{:S(2)}, u32[]{:S(2)}) %collective-permute-start.2) | collective-permute-done | bytes 393248 | tf_op jit(solution)/shard_map/ppermute | solution.py:28
  14.8 1.2 %collective-permute-done.1.rest_2_ = bf16[512,384]{1,0:T(8,128)(2,1)S(1)} collective-permute-done((bf16[512,384]{1,0:T(8,128)(2,1)S(1)}, bf16[512,384]{1,0:T(8,128)(2,1)S(1)}, u32[]{:S(2)}, u32[]{:S(2)}) %collective-permute-start.1) | collective-permute-done | bytes 393248 | tf_op jit(solution)/shard_map/ppermute | solution.py:28
  16.0 1.9 %collective-permute-start.3 = (bf16[512,384]{1,0:T(8,128)(2,1)S(1)}, bf16[512,384]{1,0:T(8,128)(2,1)S(1)}, u32[]{:S(2)}, u32[]{:S(2)}) collective-permute-start(bf16[512,384]{1,0:T(8,128)(2,1)S(1)} %broadcast_select_fusion), channel_id=1, source_target_pairs={{0,8},{8,0},{16,24},{24,16},{32,40},{40,32},{48,56},{56,48},{64,72... | collective-permute-start | bytes 1179656 | tf_op jit(solution)/shard_map/ppermute | solution.py:28
  19.2 0.0 collective-permute-done.rest_1_.kv_ref
  19.2 0.4 collective-permute-done.3.rest_4_
  19.6 1.9 %shard_map.110 = (f32[128,384]{1,0:T(8,128)S(1)}, f32[2,256,1280]{2,1,0:T(8,128)S(1)}, f32[8,2,128]{2,1,0:T(2,128)S(1)}, f32[8,128]{1,0:T(8,128)S(1)}) custom-call(s32[1,1]{1,0:T(1,128)S(6)} %copy.12.start_ref, s32[1,1]{1,0:T(1,128)S(6)} %copy.13.end_ref, bf16[128,384]{1,0:T(8,128)(2,1)S(1)} %get-tuple-element.19.q_ref, ...), custom_call_target="tpu_custom_call" | custom-call | flops 671088640 | bytes 4194304 | tf_op jit(solution)/shard_map/pallas_call | solution.py:334
  21.5 12.0 %all_to_all.10.stats_ref = f32[8,2,128]{2,1,0:T(2,128)S(1)} all-to-all(f32[8,2,128]{2,1,0:T(2,128)S(1)} %get-tuple-element.26), channel_id=1, replica_groups=mesh['dp'=2,'seq'=32,'tensor'=8] {'tensor'}, dimensions={0} | all-to-all | bytes 16384 | tf_op jit(solution)/shard_map/all_to_all | solution.py:342
  33.5 2.5 %shard_map.111 = (bf16[128,384]{1,0:T(8,128)(2,1)}, f32[32,1,384]{2,1,0:T(1,128)S(1)}, bf16[128,384]{1,0:T(8,128)(2,1)}, bf16[272,384]{1,0:T(8,128)(2,1)S(1)}) custom-call(s32[1,1]{1,0:T(1,128)S(6)} %copy.12.start_ref, s32[1,1]{1,0:T(1,128)S(6)} %copy.13.end_ref, bf16[128,384]{1,0:T(8,128)(2,1)S(1)} %get-tuple-element.19.q_ref, ...), custom_call_target="tpu_custom_call" | custom-call | flops 671088640 | bytes 4194304 | tf_op jit(solution)/shard_map/pallas_call | solution.py:343
  35.9 1.3 %collective-permute-start.5 = (bf16[272,384]{1,0:T(8,128)(2,1)S(1)}, bf16[272,384]{1,0:T(8,128)(2,1)S(1)}, u32[]{:S(2)}, u32[]{:S(2)}) collective-permute-start(bf16[272,384]{1,0:T(8,128)(2,1)S(1)} %get-tuple-element.29.sent_ref), channel_id=1, source_target_pairs={{16,0},{24,8},{32,16},{40,24},{48,32},{56,40},{64,48},{72,56},{80,... | collective-permute-start | bytes 626696 | tf_op jit(solution)/shard_map/ppermute | solution.py:28
  37.2 5.0 %collective-permute-start.4 = (bf16[272,384]{1,0:T(8,128)(2,1)S(1)}, bf16[272,384]{1,0:T(8,128)(2,1)S(1)}, u32[]{:S(2)}, u32[]{:S(2)}) collective-permute-start(bf16[272,384]{1,0:T(8,128)(2,1)S(1)} %get-tuple-element.29.sent_ref), channel_id=1, source_target_pairs={{0,16},{8,24},{16,32},{24,40},{32,48},{40,56},{48,64},{56,72},{64,... | collective-permute-start | bytes 626696 | tf_op jit(solution)/shard_map/ppermute | solution.py:28
  42.3 2.4 %collective-permute-done.5.above_ref = bf16[272,384]{1,0:T(8,128)(2,1)S(1)} collective-permute-done((bf16[272,384]{1,0:T(8,128)(2,1)S(1)}, bf16[272,384]{1,0:T(8,128)(2,1)S(1)}, u32[]{:S(2)}, u32[]{:S(2)}) %collective-permute-start.5) | collective-permute-done | bytes 208928 | tf_op jit(solution)/shard_map/ppermute | solution.py:28
  44.6 1.2 %collective-permute-done.4.below_ref = bf16[272,384]{1,0:T(8,128)(2,1)S(1)} collective-permute-done((bf16[272,384]{1,0:T(8,128)(2,1)S(1)}, bf16[272,384]{1,0:T(8,128)(2,1)S(1)}, u32[]{:S(2)}, u32[]{:S(2)}) %collective-permute-start.4) | collective-permute-done | bytes 208928 | tf_op jit(solution)/shard_map/ppermute | solution.py:28
  45.8 0.9 %shard_map.112 = bf16[512,384]{1,0:T(8,128)(2,1)S(1)} custom-call(bf16[512,384]{1,0:T(8,128)(2,1)S(1)} %collective-permute-done.rest_1_.kv_ref, bf16[272,384]{1,0:T(8,128)(2,1)S(1)} %get-tuple-element.29.sent_ref, bf16[272,384]{1,0:T(8,128)(2,1)S(1)} %collective-permute-done.4.below_ref, bf16[272,384]{1,0:T(8,128)(2,1)S(1)} %collective-permute-done.5.above_ref), custom_call_target="tpu_custom_call" | custom-call | flops 671088640 | bytes 4194304 | tf_op jit(solution)/shard_map/pallas_call | solution.py:354
  46.8 1.9 %collective-permute-start.6 = (bf16[512,384]{1,0:T(8,128)(2,1)S(1)}, bf16[512,384]{1,0:T(8,128)(2,1)S(1)}, u32[]{:S(2)}, u32[]{:S(2)}) collective-permute-start(bf16[512,384]{1,0:T(8,128)(2,1)S(1)} %shard_map.112), channel_id=1, source_target_pairs={{0,8},{8,0},{16,24},{24,16},{32,40},{40,32},{48,56},{56,48},{64,72... | collective-permute-start | bytes 1179656 | tf_op jit(solution)/shard_map/ppermute | solution.py:28
  48.7 32.0 %all_to_all.11 = f32[32,1,384]{2,1,0:T(1,128)S(1)} all-to-all(f32[32,1,384]{2,1,0:T(1,128)S(1)} %get-tuple-element.32), channel_id=1, replica_groups=mesh['dp'=2,'seq'=32,'tensor'=8] {'seq'}, dimensions={0} | all-to-all | bytes 98304 | tf_op jit(solution)/shard_map/all_to_all | solution.py:351
  80.7 0.1 reduce_sum.9
  80.8 2.5 %collective-permute-start.7 = (f32[384]{0:T(512)S(1)}, f32[384]{0:T(512)S(1)}, u32[]{:S(2)}, u32[]{:S(2)}) collective-permute-start(f32[384]{0:T(512)S(1)} %reduce_sum.9), channel_id=1, source_target_pairs={{0,256},{256,0},{1,257},{257,1},{2,258},{258,2},{3,259},{259,3},{4... | collective-permute-start | bytes 4616 | tf_op jit(solution)/shard_map/ppermute | solution.py:358
  83.3 3.0 %collective-permute-done.7 = f32[384]{0:T(512)S(1)} collective-permute-done((f32[384]{0:T(512)S(1)}, f32[384]{0:T(512)S(1)}, u32[]{:S(2)}, u32[]{:S(2)}) %collective-permute-start.7) | collective-permute-done | bytes 1568 | tf_op jit(solution)/shard_map/ppermute | solution.py:358
  86.3 0.6 add.3
  86.8 0.0 collective-permute-done.6.more_ref
  86.9 2.1 %shard_map.113 = (bf16[256,384]{1,0:T(8,128)(2,1)}, bf16[256,384]{1,0:T(8,128)(2,1)}) custom-call(bf16[512,384]{1,0:T(8,128)(2,1)S(1)} %get-tuple-element.22.rest_0_.kv_ref, bf16[272,384]{1,0:T(8,128)(2,1)S(1)} %get-tuple-element.29.sent_ref, bf16[272,384]{1,0:T(8,128)(2,1)S(1)} %collective-permute-done.4.below_ref, ...), custom_call_target="tpu_custom_call" | custom-call | flops 671088640 | bytes 4194304 | tf_op jit(solution)/shard_map/pallas_call | solution.py:359
  (1 shorter events, 0.0 us)
Async XLA Ops:
  1.8 12.9 %collective-permute-start.2 = (bf16[512,384]{1,0:T(8,128)(2,1)S(1)}, bf16[512,384]{1,0:T(8,128)(2,1)S(1)}, u32[]{:S(2)}, u32[]{:S(2)}) collective-permute-start(bf16[512,384]{1,0:T(8,128)(2,1)S(1)} %get-tuple-element.22.rest_0_.kv_ref), channel_id=1, source_target_pairs={{16,0},{24,8},{32,16},{40,24},{48,32},{56,40},{64,48},{72,56},{80,... | collective-permute-start | bytes 1179656 | tf_op jit(solution)/shard_map/ppermute | solution.py:28
  3.1 12.8 %collective-permute-start.1 = (bf16[512,384]{1,0:T(8,128)(2,1)S(1)}, bf16[512,384]{1,0:T(8,128)(2,1)S(1)}, u32[]{:S(2)}, u32[]{:S(2)}) collective-permute-start(bf16[512,384]{1,0:T(8,128)(2,1)S(1)} %get-tuple-element.22.rest_0_.kv_ref), channel_id=1, source_target_pairs={{0,16},{8,24},{16,32},{24,40},{32,48},{40,56},{48,64},{56,72},{64,... | collective-permute-start | bytes 1179656 | tf_op jit(solution)/shard_map/ppermute | solution.py:28
  7.7 11.5 %collective-permute-start = (bf16[512,384]{1,0:T(8,128)(2,1)S(1)}, bf16[512,384]{1,0:T(8,128)(2,1)S(1)}, u32[]{:S(2)}, u32[]{:S(2)}) collective-permute-start(bf16[512,384]{1,0:T(8,128)(2,1)S(1)} %get-tuple-element.22.rest_0_.kv_ref), channel_id=1, source_target_pairs={{0,8},{8,0},{16,24},{24,16},{32,40},{40,32},{48,56},{56,48},{64,72... | collective-permute-start | bytes 1179656 | tf_op jit(solution)/shard_map/ppermute | solution.py:28
  16.0 3.6 %collective-permute-start.3 = (bf16[512,384]{1,0:T(8,128)(2,1)S(1)}, bf16[512,384]{1,0:T(8,128)(2,1)S(1)}, u32[]{:S(2)}, u32[]{:S(2)}) collective-permute-start(bf16[512,384]{1,0:T(8,128)(2,1)S(1)} %broadcast_select_fusion), channel_id=1, source_target_pairs={{0,8},{8,0},{16,24},{24,16},{32,40},{40,32},{48,56},{56,48},{64,72... | collective-permute-start | bytes 1179656 | tf_op jit(solution)/shard_map/ppermute | solution.py:28
  35.9 8.7 %collective-permute-start.5 = (bf16[272,384]{1,0:T(8,128)(2,1)S(1)}, bf16[272,384]{1,0:T(8,128)(2,1)S(1)}, u32[]{:S(2)}, u32[]{:S(2)}) collective-permute-start(bf16[272,384]{1,0:T(8,128)(2,1)S(1)} %get-tuple-element.29.sent_ref), channel_id=1, source_target_pairs={{16,0},{24,8},{32,16},{40,24},{48,32},{56,40},{64,48},{72,56},{80,... | collective-permute-start | bytes 626696 | tf_op jit(solution)/shard_map/ppermute | solution.py:28
  37.2 8.6 %collective-permute-start.4 = (bf16[272,384]{1,0:T(8,128)(2,1)S(1)}, bf16[272,384]{1,0:T(8,128)(2,1)S(1)}, u32[]{:S(2)}, u32[]{:S(2)}) collective-permute-start(bf16[272,384]{1,0:T(8,128)(2,1)S(1)} %get-tuple-element.29.sent_ref), channel_id=1, source_target_pairs={{0,16},{8,24},{16,32},{24,40},{32,48},{40,56},{48,64},{56,72},{64,... | collective-permute-start | bytes 626696 | tf_op jit(solution)/shard_map/ppermute | solution.py:28
  46.8 40.1 %collective-permute-start.6 = (bf16[512,384]{1,0:T(8,128)(2,1)S(1)}, bf16[512,384]{1,0:T(8,128)(2,1)S(1)}, u32[]{:S(2)}, u32[]{:S(2)}) collective-permute-start(bf16[512,384]{1,0:T(8,128)(2,1)S(1)} %shard_map.112), channel_id=1, source_target_pairs={{0,8},{8,0},{16,24},{24,16},{32,40},{40,32},{48,56},{56,48},{64,72... | collective-permute-start | bytes 1179656 | tf_op jit(solution)/shard_map/ppermute | solution.py:28
  80.8 5.5 %collective-permute-start.7 = (f32[384]{0:T(512)S(1)}, f32[384]{0:T(512)S(1)}, u32[]{:S(2)}, u32[]{:S(2)}) collective-permute-start(f32[384]{0:T(512)S(1)} %reduce_sum.9), channel_id=1, source_target_pairs={{0,256},{256,0},{1,257},{257,1},{2,258},{258,2},{3,259},{259,3},{4... | collective-permute-start | bytes 4616 | tf_op jit(solution)/shard_map/ppermute | solution.py:358

commit v6 on v5

--- a/solution.py
+++ b/solution.py
@@ -173,9 +173,7 @@
     gain = gain_ref[...]
     normed = attn_ref[...] * inv
     attended_ref[...] = (normed * gain).astype(jnp.bfloat16)
-    gain_part_ref[...] = jnp.broadcast_to(
-        jnp.sum(grad * normed, axis=0, keepdims=True)[None], (SEQ, 1, W)
-    )
+    gain_part_ref[...] = jnp.sum(grad * normed, axis=0, keepdims=True)
     grad_attn = (inv * (grad * gain - normed * mean_cross)).astype(jnp.bfloat16)
     rows = q_ref[...]
     sent_ref[0:TB] = grad_attn
@@ -214,6 +212,10 @@
     sent_ref[2 * TB : 2 * TB + 16] = split(
         jnp.concatenate([norms_ref[...], to_rows(inners)[0:4], band], axis=0)
     )
+
+
+def spread_kernel(mine_ref, other_ref, out_ref):
+    out_ref[...] = jnp.broadcast_to((mine_ref[...] + other_ref[...])[None], (SEQ, 1, W))
 
 
 def frame_sums(kv_ref, here, tokens):
@@ -342,24 +344,24 @@
     stats = lax.all_to_all(stats, "tensor", 0, 0, tiled=False)
     attended, gain_part, grad_queries, sent = call(
         token_kernel,
-        (((TB, W), bf16), ((SEQ, 1, W), f32), ((TB, W), bf16), ((2 * TB + 16, W), bf16)),
+        (((TB, W), bf16), ((1, W), f32), ((TB, W), bf16), ((2 * TB + 16, W), bf16)),
         2,
         scratch=(whole,),
         scalars=2,
         vectors=7 + PIECES,
     )(band_start, band_end, query, grad, gain_row, attn, probs, norms, stats, *pieces)
-    spread = lax.all_to_all(gain_part, "seq", 0, 0, tiled=False)
-    gain_sum = jnp.sum(spread, axis=(0, 1))
+    gain_other = lax.ppermute(gain_part, "dp", [(0, 1), (1, 0)])
     tokens = (sent, permute(sent, "seq", lambda i: i + 2), permute(sent, "seq", lambda i: i - 2))
+    (gain_both,) = call(spread_kernel, (((SEQ, 1, W), f32),), 0, vectors=2)(gain_part, gain_other)
+    spread = lax.all_to_all(gain_both, "seq", 0, 0, tiled=False)
     (to_partner,) = call(
         partner_frame_kernel, (((2 * FR, W), bf16),), 2, vectors=4
     )(partner, *tokens)
     from_partner = permute(to_partner, "seq", lambda i: i ^ 1)
-    gain_other = lax.ppermute(gain_sum, "dp", [(0, 1), (1, 0)])
     grad_keys, grad_values = call(
         own_frame_kernel, (((FR, W), bf16), ((FR, W), bf16)), 2, vectors=5
     )(own, *tokens, from_partner)
-    grad_gain = gain_sum + gain_other
+    grad_gain = jnp.sum(spread, axis=(0, 1))
     return (
         attended[None],
         grad_queries[None],

time: 90.7 us -> 91.4 us (level)
  the two profiles are of different devices: /device:TPU:6 before, /device:TPU:1 now
where the time goes in v6:
time: 91.4 us; the launch traced here: 91 us
  blocking collectives  42.2 us (46%)
  starting transfers between devices  32.6 us (36%)
  Pallas kernels  8.59 us (9%)
  waiting for transfers between devices  4.85 us (5%)
  between operations  2.05 us (2%)
    all_to_all x1, blocking collectives, per_device(): spread = lax.all_to_all(gain_both, 'seq', 0, 0, tiled=False)  31.6 us
    ppermute x7, starting transfers between devices, permute(): return lax.ppermute(array, axis, pairs)  30.4 us
    all_to_all x1, blocking collectives, per_device(): stats = lax.all_to_all(stats, 'tensor', 0, 0, tiled=False)  10.6 us
    ppermute x7, waiting for transfers between devices, permute(): return lax.ppermute(array, axis, pairs)  2.75 us
    pallas_call x1, Pallas kernels, per_device(): call(token_kernel, (((TB, W), bf16), ((1, W), f32), ((TB, W), bf16), ((2...  2.45 us
    ppermute x1, starting transfers between devices, per_device(): gain_other = lax.ppermute(gain_part, 'dp', [(0, 1), (1, 0)])  2.22 us
    pallas_call x1, Pallas kernels, per_device(): call(own_frame_kernel, (((FR, W), bf16), ((FR, W), bf16)), 2, vectors=5)  2.11 us
    ppermute x1, waiting for transfers between devices, per_device(): gain_other = lax.ppermute(gain_part, 'dp', [(0, 1), (1, 0)])  2.1 us
  transfers between devices with their start and end apart: 8, of which 3 were waited for; matrix products, arithmetic and copies ran while one was open for 1% of the time, Pallas kernels for 0%

profile of v6, /device:TPU:1, one launch (start us, length us, event | category | flops | bytes accessed | tf_op | source)
XLA Modules:
  0.0 91.0 jit_solution(17389035970731529396)
XLA Ops:
  0.6 1.2 %pack.1 = (bf16[512,384]{1,0:T(8,128)(2,1)S(1)}, bf16[128,384]{1,0:T(8,128)(2,1)S(1)}, bf16[128,384]{1,0:T(8,128)(2,1)S(1)}, f32[1,384]{1,0:T(1,128)S(1)}) custom-call(bf16[256,384]{1,0:T(8,128)(2,1)} %bitcast.8, bf16[256,384]{1,0:T(8,128)(2,1)} %bitcast.9, bf16[128,384]{1,0:T(8,128)(2,1)} %bitcast.10, bf16[128,384]{1,0:T(8,128)(2,1)} %bitcast.11, f32[384]{0:T(512)} %gain_ref.1), custom_call_target="tpu_custom_call" | custom-call | tf_op jit(solution)/shard_map/pack/pallas_call | solution.py:313
  1.8 1.3 %collective-permute-start.2 = (bf16[512,384]{1,0:T(8,128)(2,1)S(1)}, bf16[512,384]{1,0:T(8,128)(2,1)S(1)}, u32[]{:S(2)}, u32[]{:S(2)}) collective-permute-start(bf16[512,384]{1,0:T(8,128)(2,1)S(1)} %get-tuple-element.22.rest_0_.kv_ref), channel_id=1, source_target_pairs={{16,0},{24,8},{32,16},{40,24},{48,32},{56,40},{64,48},{72,56},{80,... | collective-permute-start | bytes 1179656 | tf_op jit(solution)/shard_map/ppermute | solution.py:28
  3.1 5.0 %collective-permute-start.1 = (bf16[512,384]{1,0:T(8,128)(2,1)S(1)}, bf16[512,384]{1,0:T(8,128)(2,1)S(1)}, u32[]{:S(2)}, u32[]{:S(2)}) collective-permute-start(bf16[512,384]{1,0:T(8,128)(2,1)S(1)} %get-tuple-element.22.rest_0_.kv_ref), channel_id=1, source_target_pairs={{0,16},{8,24},{16,32},{24,40},{32,48},{40,56},{48,64},{56,72},{64,... | collective-permute-start | bytes 1179656 | tf_op jit(solution)/shard_map/ppermute | solution.py:28
  8.1 8.3 %collective-permute-start = (bf16[512,384]{1,0:T(8,128)(2,1)S(1)}, bf16[512,384]{1,0:T(8,128)(2,1)S(1)}, u32[]{:S(2)}, u32[]{:S(2)}) collective-permute-start(bf16[512,384]{1,0:T(8,128)(2,1)S(1)} %get-tuple-element.22.rest_0_.kv_ref), channel_id=1, source_target_pairs={{0,8},{8,0},{16,24},{24,16},{32,40},{40,32},{48,56},{56,48},{64,72... | collective-permute-start | bytes 1179656 | tf_op jit(solution)/shard_map/ppermute | solution.py:28
  16.5 0.0 collective-permute-done.2.rest_3_
  16.5 0.0 collective-permute-done.1.rest_2_
  16.5 0.1 broadcast_select_fusion
  16.5 5.2 %collective-permute-start.3 = (bf16[512,384]{1,0:T(8,128)(2,1)S(1)}, bf16[512,384]{1,0:T(8,128)(2,1)S(1)}, u32[]{:S(2)}, u32[]{:S(2)}) collective-permute-start(bf16[512,384]{1,0:T(8,128)(2,1)S(1)} %broadcast_select_fusion), channel_id=1, source_target_pairs={{0,8},{8,0},{16,24},{24,16},{32,40},{40,32},{48,56},{56,48},{64,72... | collective-permute-start | bytes 1179656 | tf_op jit(solution)/shard_map/ppermute | solution.py:28
  23.1 0.0 collective-permute-done.rest_1_.kv_ref
  23.1 0.0 collective-permute-done.3.rest_4_
  23.1 1.9 %shard_map.110 = (f32[128,384]{1,0:T(8,128)S(1)}, f32[2,256,1280]{2,1,0:T(8,128)S(1)}, f32[8,2,128]{2,1,0:T(2,128)S(1)}, f32[8,128]{1,0:T(8,128)S(1)}) custom-call(s32[1,1]{1,0:T(1,128)S(6)} %copy.12.start_ref, s32[1,1]{1,0:T(1,128)S(6)} %copy.13.end_ref, bf16[128,384]{1,0:T(8,128)(2,1)S(1)} %get-tuple-element.19.q_ref, ...), custom_call_target="tpu_custom_call" | custom-call | flops 671088640 | bytes 4194304 | tf_op jit(solution)/shard_map/pallas_call | solution.py:336
  25.0 10.6 %all_to_all.10.stats_ref = f32[8,2,128]{2,1,0:T(2,128)S(1)} all-to-all(f32[8,2,128]{2,1,0:T(2,128)S(1)} %get-tuple-element.26), channel_id=1, replica_groups=mesh['dp'=2,'seq'=32,'tensor'=8] {'tensor'}, dimensions={0} | all-to-all | bytes 16384 | tf_op jit(solution)/shard_map/all_to_all | solution.py:344
  35.6 2.5 %shard_map.111 = (bf16[128,384]{1,0:T(8,128)(2,1)}, f32[1,384]{1,0:T(1,128)S(1)}, bf16[128,384]{1,0:T(8,128)(2,1)}, bf16[272,384]{1,0:T(8,128)(2,1)S(1)}) custom-call(s32[1,1]{1,0:T(1,128)S(6)} %copy.12.start_ref, s32[1,1]{1,0:T(1,128)S(6)} %copy.13.end_ref, bf16[128,384]{1,0:T(8,128)(2,1)S(1)} %get-tuple-element.19.q_ref, ...), custom_call_target="tpu_custom_call" | custom-call | flops 671088640 | bytes 4194304 | tf_op jit(solution)/shard_map/pallas_call | solution.py:345
  38.1 1.3 %collective-permute-start.5 = (bf16[272,384]{1,0:T(8,128)(2,1)S(1)}, bf16[272,384]{1,0:T(8,128)(2,1)S(1)}, u32[]{:S(2)}, u32[]{:S(2)}) collective-permute-start(bf16[272,384]{1,0:T(8,128)(2,1)S(1)} %get-tuple-element.29.sent_ref), channel_id=1, source_target_pairs={{16,0},{24,8},{32,16},{40,24},{48,32},{56,40},{64,48},{72,56},{80,... | collective-permute-start | bytes 626696 | tf_op jit(solution)/shard_map/ppermute | solution.py:28
  39.3 4.7 %collective-permute-start.4 = (bf16[272,384]{1,0:T(8,128)(2,1)S(1)}, bf16[272,384]{1,0:T(8,128)(2,1)S(1)}, u32[]{:S(2)}, u32[]{:S(2)}) collective-permute-start(bf16[272,384]{1,0:T(8,128)(2,1)S(1)} %get-tuple-element.29.sent_ref), channel_id=1, source_target_pairs={{0,16},{8,24},{16,32},{24,40},{32,48},{40,56},{48,64},{56,72},{64,... | collective-permute-start | bytes 626696 | tf_op jit(solution)/shard_map/ppermute | solution.py:28
  44.1 1.8 %collective-permute-done.5.above_ref = bf16[272,384]{1,0:T(8,128)(2,1)S(1)} collective-permute-done((bf16[272,384]{1,0:T(8,128)(2,1)S(1)}, bf16[272,384]{1,0:T(8,128)(2,1)S(1)}, u32[]{:S(2)}, u32[]{:S(2)}) %collective-permute-start.5) | collective-permute-done | bytes 208928 | tf_op jit(solution)/shard_map/ppermute | solution.py:28
  45.9 0.9 %collective-permute-done.4.below_ref = bf16[272,384]{1,0:T(8,128)(2,1)S(1)} collective-permute-done((bf16[272,384]{1,0:T(8,128)(2,1)S(1)}, bf16[272,384]{1,0:T(8,128)(2,1)S(1)}, u32[]{:S(2)}, u32[]{:S(2)}) %collective-permute-start.4) | collective-permute-done | bytes 208928 | tf_op jit(solution)/shard_map/ppermute | solution.py:28
  46.8 0.9 %shard_map.112 = bf16[512,384]{1,0:T(8,128)(2,1)S(1)} custom-call(bf16[512,384]{1,0:T(8,128)(2,1)S(1)} %collective-permute-done.rest_1_.kv_ref, bf16[272,384]{1,0:T(8,128)(2,1)S(1)} %get-tuple-element.29.sent_ref, bf16[272,384]{1,0:T(8,128)(2,1)S(1)} %collective-permute-done.4.below_ref, bf16[272,384]{1,0:T(8,128)(2,1)S(1)} %collective-permute-done.5.above_ref), custom_call_target="tpu_custom_call" | custom-call | flops 671088640 | bytes 4194304 | tf_op jit(solution)/shard_map/pallas_call | solution.py:357
  47.8 4.6 %collective-permute-start.6 = (bf16[512,384]{1,0:T(8,128)(2,1)S(1)}, bf16[512,384]{1,0:T(8,128)(2,1)S(1)}, u32[]{:S(2)}, u32[]{:S(2)}) collective-permute-start(bf16[512,384]{1,0:T(8,128)(2,1)S(1)} %shard_map.112), channel_id=1, source_target_pairs={{0,8},{8,0},{16,24},{24,16},{32,40},{40,32},{48,56},{56,48},{64,72... | collective-permute-start | bytes 1179656 | tf_op jit(solution)/shard_map/ppermute | solution.py:28
  52.3 2.2 %collective-permute-start.7 = (f32[1,384]{1,0:T(1,128)S(1)}, f32[1,384]{1,0:T(1,128)S(1)}, u32[]{:S(2)}, u32[]{:S(2)}) collective-permute-start(f32[1,384]{1,0:T(1,128)S(1)} %get-tuple-element.32.mine_ref), channel_id=1, source_target_pairs={{0,256},{256,0},{1,257},{257,1},{2,258},{258,2},{3,259},{259,3},{4... | collective-permute-start | bytes 4616 | tf_op jit(solution)/shard_map/ppermute | solution.py:353
  54.6 2.1 %collective-permute-done.7.other_ref = f32[1,384]{1,0:T(1,128)S(1)} collective-permute-done((f32[1,384]{1,0:T(1,128)S(1)}, f32[1,384]{1,0:T(1,128)S(1)}, u32[]{:S(2)}, u32[]{:S(2)}) %collective-permute-start.7) | collective-permute-done | bytes 1568 | tf_op jit(solution)/shard_map/ppermute | solution.py:353
  56.7 31.6 %all_to_all.11 = f32[32,1,384]{2,1,0:T(1,128)S(1)} all-to-all(f32[32,1,384]{2,1,0:T(1,128)S(1)} %shard_map.114), channel_id=1, replica_groups=mesh['dp'=2,'seq'=32,'tensor'=8] {'seq'}, dimensions={0} | all-to-all | bytes 98304 | tf_op jit(solution)/shard_map/all_to_all | solution.py:356
  88.3 0.6 reduce_sum.9
  88.9 0.0 collective-permute-done.6.more_ref
  88.9 2.1 %shard_map.113 = (bf16[256,384]{1,0:T(8,128)(2,1)}, bf16[256,384]{1,0:T(8,128)(2,1)}) custom-call(bf16[512,384]{1,0:T(8,128)(2,1)S(1)} %get-tuple-element.22.rest_0_.kv_ref, bf16[272,384]{1,0:T(8,128)(2,1)S(1)} %get-tuple-element.29.sent_ref, bf16[272,384]{1,0:T(8,128)(2,1)S(1)} %collective-permute-done.4.below_ref, ...), custom_call_target="tpu_custom_call" | custom-call | flops 671088640 | bytes 4194304 | tf_op jit(solution)/shard_map/pallas_call | solution.py:361
  (1 shorter events, 0.0 us)
Async XLA Ops:
  1.8 14.6 %collective-permute-start.2 = (bf16[512,384]{1,0:T(8,128)(2,1)S(1)}, bf16[512,384]{1,0:T(8,128)(2,1)S(1)}, u32[]{:S(2)}, u32[]{:S(2)}) collective-permute-start(bf16[512,384]{1,0:T(8,128)(2,1)S(1)} %get-tuple-element.22.rest_0_.kv_ref), channel_id=1, source_target_pairs={{16,0},{24,8},{32,16},{40,24},{48,32},{56,40},{64,48},{72,56},{80,... | collective-permute-start | bytes 1179656 | tf_op jit(solution)/shard_map/ppermute | solution.py:28
  3.1 13.4 %collective-permute-start.1 = (bf16[512,384]{1,0:T(8,128)(2,1)S(1)}, bf16[512,384]{1,0:T(8,128)(2,1)S(1)}, u32[]{:S(2)}, u32[]{:S(2)}) collective-permute-start(bf16[512,384]{1,0:T(8,128)(2,1)S(1)} %get-tuple-element.22.rest_0_.kv_ref), channel_id=1, source_target_pairs={{0,16},{8,24},{16,32},{24,40},{32,48},{40,56},{48,64},{56,72},{64,... | collective-permute-start | bytes 1179656 | tf_op jit(solution)/shard_map/ppermute | solution.py:28
  8.1 14.9 %collective-permute-start = (bf16[512,384]{1,0:T(8,128)(2,1)S(1)}, bf16[512,384]{1,0:T(8,128)(2,1)S(1)}, u32[]{:S(2)}, u32[]{:S(2)}) collective-permute-start(bf16[512,384]{1,0:T(8,128)(2,1)S(1)} %get-tuple-element.22.rest_0_.kv_ref), channel_id=1, source_target_pairs={{0,8},{8,0},{16,24},{24,16},{32,40},{40,32},{48,56},{56,48},{64,72... | collective-permute-start | bytes 1179656 | tf_op jit(solution)/shard_map/ppermute | solution.py:28
  16.5 6.5 %collective-permute-start.3 = (bf16[512,384]{1,0:T(8,128)(2,1)S(1)}, bf16[512,384]{1,0:T(8,128)(2,1)S(1)}, u32[]{:S(2)}, u32[]{:S(2)}) collective-permute-start(bf16[512,384]{1,0:T(8,128)(2,1)S(1)} %broadcast_select_fusion), channel_id=1, source_target_pairs={{0,8},{8,0},{16,24},{24,16},{32,40},{40,32},{48,56},{56,48},{64,72... | collective-permute-start | bytes 1179656 | tf_op jit(solution)/shard_map/ppermute | solution.py:28
  38.1 7.8 %collective-permute-start.5 = (bf16[272,384]{1,0:T(8,128)(2,1)S(1)}, bf16[272,384]{1,0:T(8,128)(2,1)S(1)}, u32[]{:S(2)}, u32[]{:S(2)}) collective-permute-start(bf16[272,384]{1,0:T(8,128)(2,1)S(1)} %get-tuple-element.29.sent_ref), channel_id=1, source_target_pairs={{16,0},{24,8},{32,16},{40,24},{48,32},{56,40},{64,48},{72,56},{80,... | collective-permute-start | bytes 626696 | tf_op jit(solution)/shard_map/ppermute | solution.py:28
  39.3 7.5 %collective-permute-start.4 = (bf16[272,384]{1,0:T(8,128)(2,1)S(1)}, bf16[272,384]{1,0:T(8,128)(2,1)S(1)}, u32[]{:S(2)}, u32[]{:S(2)}) collective-permute-start(bf16[272,384]{1,0:T(8,128)(2,1)S(1)} %get-tuple-element.29.sent_ref), channel_id=1, source_target_pairs={{0,16},{8,24},{16,32},{24,40},{32,48},{40,56},{48,64},{56,72},{64,... | collective-permute-start | bytes 626696 | tf_op jit(solution)/shard_map/ppermute | solution.py:28
  47.8 41.1 %collective-permute-start.6 = (bf16[512,384]{1,0:T(8,128)(2,1)S(1)}, bf16[512,384]{1,0:T(8,128)(2,1)S(1)}, u32[]{:S(2)}, u32[]{:S(2)}) collective-permute-start(bf16[512,384]{1,0:T(8,128)(2,1)S(1)} %shard_map.112), channel_id=1, source_target_pairs={{0,8},{8,0},{16,24},{24,16},{32,40},{40,32},{48,56},{56,48},{64,72... | collective-permute-start | bytes 1179656 | tf_op jit(solution)/shard_map/ppermute | solution.py:28
  52.3 4.3 %collective-permute-start.7 = (f32[1,384]{1,0:T(1,128)S(1)}, f32[1,384]{1,0:T(1,128)S(1)}, u32[]{:S(2)}, u32[]{:S(2)}) collective-permute-start(f32[1,384]{1,0:T(1,128)S(1)} %get-tuple-element.32.mine_ref), channel_id=1, source_target_pairs={{0,256},{256,0},{1,257},{257,1},{2,258},{258,2},{3,259},{259,3},{4... | collective-permute-start | bytes 4616 | tf_op jit(solution)/shard_map/ppermute | solution.py:353
